TPU v7x, 32 devices: a whole 2x2x4 slice. The times are simulated.
32 devices in a mesh: parts: 2 (over y), blk: 4 (over z), users: 2 (over x), sub: 2 (over core).
Axes of the slice: x: 2, y: 2, z: 4, core: 2. Of those that a mesh axis runs over, the one named last changes fastest.
Arguments:
- history: bfloat16 [64, 64, 256], P(('parts', 'blk'), 'users'), parts along dimension 0, may hold values from -400 to 400
- lengths: int32 [64], P(('parts', 'blk')), parts along dimension 0, may hold values from 1 to 64
- item_rows: bfloat16 [12288, 512], P(('parts', 'blk', 'users', 'sub')), parts along dimension 0, may hold values from -6 to 6
- w_query: bfloat16 [512, 256], replicated, may hold values from -0.25 to 0.25
- w_item: bfloat16 [512, 256], replicated, may hold values from -0.25 to 0.25
- w_key: bfloat16 [256, 256], replicated, may hold values from -0.375 to 0.375
- w_value: bfloat16 [256, 256], replicated, may hold values from -0.375 to 0.375
- w_pooled: bfloat16 [256, 128], replicated, may hold values from -0.25 to 0.25
- w_joint: bfloat16 [256, 128], replicated, may hold values from -0.25 to 0.25
- bias_hidden: float32 [128], replicated, may hold values from -3 to 3
- w_task: bfloat16 [128, 8], replicated, may hold values from -0.5 to 0.5
- bias_task: float32 [8], replicated, may hold values from -3 to 3
Outputs:
- logits: float32 [64, 9, 8, 1536], P(('parts', 'blk'), None, None, ('users', 'sub')), parts along dimension 0
There are 2 independent parts, one for each index of `parts`. A program takes and returns all parts, laid end to end along the dimension named above; an argument that names none is the same for every part. Nothing has to cross between parts.
All inputs are finite; a program needn't handle non-finite values.
Results may differ from a plain program's by a relative error of at most 0.011.
Values may be sent and summed in bfloat16 or wider, within the bound.
No kernel may reach another device: no remote copies, remote signals or barrier semaphores. Data moves between devices by JAX's collectives and lax.ppermute only.
A program may use at most 64 MiB of HBM per device.

v0:
```python
import functools
import math

import jax
import jax.numpy as jnp
from jax import lax
from jax.experimental import pallas as pl
from jax.experimental.pallas import tpu as pltpu
from jax.sharding import PartitionSpec as P


REACH = 4
WIN = 2 * REACH + 1
LENGTH_ROWS = 8
KERNEL_BYTES = 16 << 20
BF16 = jnp.bfloat16
F32 = jnp.float32
VMEM = pl.BlockSpec(memory_space=pltpu.VMEM)
SMEM = pl.BlockSpec(memory_space=pltpu.SMEM)
HBM = pl.BlockSpec(memory_space=pltpu.HBM)


def call(kernel, out_shape, in_specs, out_specs, args, flops, scratch=(), aliases=None):
    moved = sum(math.prod(a.shape) * a.dtype.itemsize for a in args)
    spaces = {id(VMEM): pltpu.VMEM, id(HBM): pltpu.HBM}
    args = [pltpu.with_memory_space_constraint(a, spaces[id(spec)]) for a, spec in zip(args, in_specs)]
    return pl.pallas_call(
        kernel,
        out_shape=out_shape,
        in_specs=in_specs,
        out_specs=out_specs,
        scratch_shapes=list(scratch),
        input_output_aliases=aliases or {},
        compiler_params=pltpu.CompilerParams(vmem_limit_bytes=KERNEL_BYTES),
        cost_estimate=pl.CostEstimate(flops=flops, bytes_accessed=moved, transcendentals=0),
    )(*args)


def pack_kernel(shares, history_ref, lengths_ref, piece_ref, held_ref, sems):
    users, tokens, _ = history_ref.shape
    users //= shares
    width = piece_ref.shape[1]
    first = lax.axis_index("sub") * users
    copies = [pltpu.make_async_copy(lengths_ref, held_ref, sems.at[users])]
    for user in range(users):
        place = piece_ref.at[pl.ds(user * tokens, tokens)]
        copies.append(pltpu.make_async_copy(history_ref.at[first + user], place, sems.at[user]))
    for copy in copies:
        copy.start()
    copies[0].wait()
    row = lax.broadcasted_iota(jnp.int32, (LENGTH_ROWS, width), 0)
    lengths = jnp.zeros((LENGTH_ROWS, width), F32)
    for user in range(users):
        lengths = jnp.where(row == user, held_ref[first + user].astype(F32), lengths)
    piece_ref[users * tokens :, :] = lengths.astype(BF16)
    for copy in copies[1:]:
        copy.wait()


def project_kernel(*refs):
    sources, (out_ref, heads_ref, bias_out), held, sems = refs[:7], refs[7:10], refs[10:17], refs[17]
    copies = [pltpu.make_async_copy(*pair, sems.at[i]) for i, pair in enumerate(zip(sources, held))]
    for copy in copies:
        copy.start()
    items_ref, w_query_ref, w_item_ref, w_joint_ref, bias_ref, w_task_ref, bias_task_ref = held
    for copy in copies[5:]:
        copy.wait()
    tasks, hid = w_task_ref.shape
    w_task = w_task_ref[...].astype(F32)
    blank = jnp.zeros_like(w_task)
    heads_ref[:, :hid] = jnp.concatenate([w_task, blank], 0).astype(BF16)
    heads_ref[:, hid:] = jnp.concatenate([blank, w_task], 0).astype(BF16)
    row = lax.broadcasted_iota(jnp.int32, bias_out.shape, 0) % tasks
    bias = jnp.zeros(bias_out.shape, F32)
    for task in range(tasks):
        bias = jnp.where(row == task, bias_task_ref[task], bias)
    bias_out[...] = bias
    for copy in copies[:5]:
        copy.wait()
    width = w_query_ref.shape[1]
    rows = items_ref[...]
    queries = jnp.dot(rows, w_query_ref[...], preferred_element_type=F32)
    out_ref[:width, :] = queries.T.astype(BF16)
    joined = jnp.dot(rows, w_item_ref[...], preferred_element_type=F32).astype(BF16)
    terms = jnp.dot(joined, w_joint_ref[...], preferred_element_type=F32) + bias_ref[...]
    out_ref[width:, :] = terms.T.astype(BF16)


def keys_values(pieces, turn, w_key_ref, w_value_ref, w_pooled_ref, key_ref, pooled_ref, mask_ref, history_ref):
    pairs, hid, depth = pooled_ref.shape
    hid //= 2
    both = depth - hid
    full = both // 2
    users = 2 * pairs
    share = users // len(pieces)
    for s, parts in enumerate(pieces):
        tokens = full // len(parts)
        for r, (rows, first) in enumerate(parts):
            at = (lax.broadcasted_iota(jnp.int32, (tokens, 128), 0) + first).astype(F32)
            for u in range(share):
                start = (s * share + u) * full + r * tokens
                place = slice(start, start + tokens)
                history_ref[place, :] = rows[u * tokens : (u + 1) * tokens]
                mask_ref[place, :] = jnp.where(at < turn[s][u : u + 1, :128], 0.0, -jnp.inf)
    key_ref[...] = jnp.dot(history_ref[...], w_key_ref[...], preferred_element_type=F32).astype(BF16)
    values = jnp.dot(history_ref[...], w_value_ref[...], preferred_element_type=F32).astype(BF16)
    pooled = jnp.dot(values, w_pooled_ref[...], preferred_element_type=F32)
    lane = lax.broadcasted_iota(jnp.int32, (hid, both), 1)
    one = lax.broadcasted_iota(jnp.int32, (2 * hid, hid), 0) % hid
    one = jnp.where(one == lax.broadcasted_iota(jnp.int32, (2 * hid, hid), 1), 1.0, 0.0).astype(BF16)
    for pair in range(pairs):
        flat = pooled[pair * both : (pair + 1) * both].T
        pooled_ref[pair, :hid, :both] = jnp.where(lane < full, flat, 0.0).astype(BF16)
        pooled_ref[pair, hid:, :both] = jnp.where(lane < full, 0.0, flat).astype(BF16)
        pooled_ref[pair, :, both:] = one


def score(items_ref, state, heads_ref, bias_ref, out_ref, scratch, shares):
    key_ref, pooled_ref, mask_ref = state
    scores_ref, weights_ref, hidden_ref = scratch
    width = key_ref.shape[1]
    tasks = heads_ref.shape[0] // 2
    pairs, hid, depth = pooled_ref.shape
    both = depth - hid // 2
    full = both // 2
    share = pairs // shares
    columns = items_ref.shape[1]
    factor = math.log2(math.e) / math.sqrt(width)

    scores_ref[...] = jnp.dot(key_ref[...], items_ref[:width, :], preferred_element_type=F32)
    for user in range(2 * pairs):
        rows = slice(user * full, (user + 1) * full)
        for column in range(0, columns, 128):
            lanes = slice(column, column + 128)
            scores = scores_ref[rows, lanes] + mask_ref[rows, :]
            maximum = jnp.max(scores, axis=0, keepdims=True)
            expo = jnp.exp2((scores - maximum) * factor)
            weights = expo * (1.0 / jnp.sum(expo, axis=0, keepdims=True))
            weights_ref[rows, lanes] = weights.astype(BF16)
    for pair in range(pairs):
        rows = slice(pair * both, (pair + 1) * both)
        inputs = jnp.concatenate([weights_ref[rows, :], items_ref[width:, :]], 0)
        hidden = jnp.dot(pooled_ref[pair], inputs, preferred_element_type=F32)
        hidden_ref[pair] = jnp.maximum(hidden, 0.0).astype(BF16)
    bias = jnp.concatenate([bias_ref[...]] * (columns // 128), 1)
    for pair in range(pairs):
        logits = jnp.dot(heads_ref[...], hidden_ref[pair], preferred_element_type=F32) + bias
        first = lax.rem(lax.axis_index("sub") + pair // share, shares) * share + pair % share
        if len(out_ref.shape) == 3:
            out_ref[2 * first] = logits[:tasks]
            out_ref[2 * first + 1] = logits[tasks:]
        else:
            place = pl.multiple_of(2 * first * tasks, 2 * tasks)
            out_ref[pl.ds(place, 2 * tasks), :] = logits.astype(out_ref.dtype)


def first_kernel(own, shares, parts, *refs):
    if own:
        history_ref, refs = refs[0], refs[1:]
    given = [own and s > 0 and r == 0 and parts > 1 for s in range(shares) for r in range(parts)]
    count = given.count(False)
    sent, refs = list(refs[:count]), refs[count:]
    piece_refs = [None if local else sent.pop(0) for local in given]
    w_key_ref, w_value_ref, w_pooled_ref, items_ref, heads_ref, bias_ref = refs[:6]
    out_ref, key_ref, pooled_ref, mask_ref, rows_ref, *scratch = refs[6:]
    me, side = lax.axis_index("users"), lax.axis_index("sub")
    pieces, turn = [], []
    rows = piece_refs[0].shape[0] - LENGTH_ROWS
    tokens = (pooled_ref.shape[2] - pooled_ref.shape[1] // 2) // 2 // parts
    for s in range(shares):
        entries = []
        for r in range(parts):
            ref = piece_refs[s * parts + r]
            if own and s > 0 and r == 0:
                users = history_ref.shape[0] // shares
                chosen = history_ref[pl.ds(lax.rem(side + s, shares) * users, users)]
                content = chosen.reshape(rows, history_ref.shape[2])
            else:
                content = ref[:rows, :]
            entries.append((content, lax.rem(me + r, parts) * tokens))
        pieces.append(entries)
        turn.append(piece_refs[s * parts + parts - 1][rows:, :].astype(F32))
    state = (key_ref, pooled_ref, mask_ref)
    keys_values(pieces, turn, w_key_ref, w_value_ref, w_pooled_ref, *state, rows_ref)
    score(items_ref, state, heads_ref, bias_ref, out_ref, scratch, shares)


def next_kernel(shares, items_ref, key_ref, pooled_ref, mask_ref, heads_ref, bias_ref, out_ref, *scratch):
    state = (key_ref, pooled_ref, mask_ref)
    score(items_ref, state, heads_ref, bias_ref, out_ref, scratch, shares)


def place_own_kernel(home_ref, beside_ref, out_ref, sems):
    even = lax.rem(lax.axis_index("blk"), 2)
    places = [(home_ref, k) for k in range(0, WIN, REACH)]
    places += [(beside_ref, 1 + 2 * even), (beside_ref, 1 + 2 * even + REACH)]
    copies = [pltpu.make_async_copy(a, out_ref.at[:, k], sems.at[i]) for i, (a, k) in enumerate(places)]
    for copy in copies:
        copy.start()
    for copy in copies:
        copy.wait()


def place_away_kernel(*refs):
    *backs, _, out_ref, held, sems = refs
    _, users, tasks, _ = held.shape
    odd = 3 - 2 * lax.rem(lax.axis_index("blk"), 2)
    copies = []
    for at, (back_ref, first) in enumerate(zip(backs, (2, odd))):
        for user in range(0, users, 2):
            both = back_ref[user * tasks : (user + 2) * tasks, :].astype(F32)
            held[at, user] = both[:tasks]
            held[at, user + 1] = both[tasks:]
        for k in range(2):
            place = out_ref.at[:, first + k * REACH]
            copies.append(pltpu.make_async_copy(held.at[at], place, sems.at[2 * at + k]))
            copies[-1].start()
    for copy in copies:
        copy.wait()


def shift(block, axis, distance):
    count = lax.axis_size(axis)
    return lax.ppermute(block, axis, [((i + distance) % count, i) for i in range(count)])


def spread(piece, shares, parts, own=False):
    row = [piece]
    for r in range(1, parts):
        row.append(shift(piece, "users", r))
    table = [row]
    for s in range(1, shares):
        line = [None]
        for r in range(parts):
            if r or not own or parts == 1:
                entry = shift(row[r], "sub", s)
                line[r:] = [entry]
        table.append(line)
    return table


def shards(
    history,
    lengths,
    item_rows,
    w_query,
    w_item,
    w_key,
    w_value,
    w_pooled,
    w_joint,
    bias_hidden,
    w_task,
    bias_task,
):
    users, tokens, width = history.shape
    items = item_rows.shape[0]
    hid, tasks = w_task.shape
    count, parts, shares = (lax.axis_size(axis) for axis in ("blk", "users", "sub"))
    full = tokens * parts

    share = users // shares
    piece = call(
        functools.partial(pack_kernel, shares),
        pltpu.VMEM((share * tokens + LENGTH_ROWS, width), BF16),
        [HBM] * 2,
        VMEM,
        (history, lengths),
        0,
        (pltpu.SMEM(lengths.shape, jnp.int32), pltpu.SemaphoreType.DMA((share + 1,))),
    )
    operands = (item_rows, w_query, w_item, w_joint, bias_hidden[None], w_task.T)
    mine, heads, bias = call(
        project_kernel,
        (
            pltpu.VMEM((width + hid, items), BF16),
            pltpu.VMEM((2 * tasks, 2 * hid), BF16),
            pltpu.VMEM((2 * tasks, 128), F32),
        ),
        [HBM] * 7,
        [VMEM] * 3,
        (*operands, bias_task),
        2 * items * item_rows.shape[1] * 2 * width,
        (
            *(pltpu.VMEM(a.shape, a.dtype) for a in operands),
            pltpu.SMEM(bias_task.shape, F32),
            pltpu.SemaphoreType.DMA((7,)),
        ),
    )
    flops = 2 * users * items * (full * (width + hid) + hid * tasks)
    state = (
        pltpu.VMEM((users * full, width), BF16),
        pltpu.VMEM((users // 2, 2 * hid, 2 * full + hid), BF16),
        pltpu.VMEM((users * full, 128), F32),
    )
    kept = pltpu.VMEM((users, tasks, items), F32)
    sent = pltpu.VMEM((users * tasks, items), BF16)
    scratch = (
        pltpu.VMEM((users * full, items), F32),
        pltpu.VMEM((users * full, items), BF16),
        pltpu.VMEM((users // 2, 2 * hid, items), BF16),
    )

    def start(table, block, out, own):
        flat = [entry for row in table for entry in row if entry is not None]
        head = [history] if own else []
        result = call(
            functools.partial(first_kernel, own, shares, parts),
            (out, *state),
            [VMEM] * (len(head) + len(flat) + 6),
            [VMEM] * 4,
            (*head, *flat, w_key, w_value, w_pooled, block, heads, bias),
            flops + 4 * users * full * width * width,
            (pltpu.VMEM((users * full, width), BF16), *scratch),
        )
        return result[0], result[1:]

    def go_on(held, block, out):
        return call(
            functools.partial(next_kernel, shares),
            out,
            [VMEM] * 6,
            VMEM,
            (block, *held, heads, bias),
            flops,
            scratch,
        )

    if count != REACH:
        window = [None] * WIN
        table = spread(piece, shares, parts, True)
        window[REACH], held = start(table, mine, kept, True)
        low = high = mine
        for offset in range(1, REACH + 1):
            low, high = shift(low, "blk", -1), shift(high, "blk", 1)
            window[REACH - offset] = go_on(held, low, kept)
            window[REACH + offset] = go_on(held, high, kept)
        return jnp.stack(window, axis=1)

    across = [(i ^ 2, i) for i in range(count)]
    far = lax.ppermute(piece, "blk", across)
    other = lax.ppermute(mine, "blk", [(i ^ 1, i) for i in range(count)])
    table = spread(far, shares, parts)
    own = spread(piece, shares, parts, True)
    result, guests = start(table, mine, sent, False)
    first = lax.ppermute(result, "blk", across)
    result = go_on(guests, other, sent)
    second = lax.ppermute(result, "blk", across)
    at_home, held = start(own, mine, kept, True)
    beside = go_on(held, other, kept)
    whole = jax.ShapeDtypeStruct((users, WIN, tasks, items), F32)
    semaphores = pltpu.SemaphoreType.DMA((5,))
    out = call(place_own_kernel, whole, [VMEM] * 2, HBM, (at_home, beside), 0, (semaphores,))
    held = (pltpu.VMEM((2, users, tasks, items), F32), pltpu.SemaphoreType.DMA((4,)))
    specs = [VMEM, VMEM, HBM]
    return call(place_away_kernel, whole, specs, HBM, (first, second, out), 0, held, {2: 0})


def solution(mesh):
    placed = (
        P(("parts", "blk"), "users", None),
        P(("parts", "blk")),
        P(("parts", "blk", "users", "sub"), None),
        P(),
        P(),
        P(),
        P(),
        P(),
        P(),
        P(),
        P(),
        P(),
    )

    return jax.shard_map(
        shards,
        mesh=mesh,
        in_specs=placed,
        out_specs=P(("parts", "blk"), None, None, ("users", "sub")),
        check_vma=False,
    )
```

profile of v0, /device:TPU:0, one launch (start us, length us, event | category | flops | bytes accessed | tf_op | source)
XLA Modules:
  0.0 30.7 jit_solution(4404110748764340404)
XLA Ops:
  0.0 0.0 copy-start.2
  0.0 1.9 %shard_map.119 = (bf16[384,384]{1,0:T(8,128)(2,1)S(1)}, bf16[16,256]{1,0:T(8,128)(2,1)S(1)}, f32[16,128]{1,0:T(8,128)S(1)}) custom-call(bf16[384,512]{1,0:T(8,128)(2,1)} %refs_0_.2, bf16[512,256]{1,0:T(8,128)(2,1)} %refs_1_.1, bf16[512,256]{1,0:T(8,128)(2,1)} %refs_2_.1, bf16[256,128]{1,0:T(8,128)(2,1)} %refs_3_.1, f32[1,128]{1,0:T(1,128)} %bitcast.3, ...), custom_call_target="tpu_custom_call" | custom-call | flops 201326592 | bytes 985632 | tf_op jit(solution)/shard_map/pallas_call | solution.py:27
  1.9 0.0 copy-start.1
  1.9 0.0 copy-start.3
  1.9 3.1 %collective-permute-start.5 = (bf16[384,384]{1,0:T(8,128)(2,1)S(1)}, bf16[384,384]{1,0:T(8,128)(2,1)S(1)}, u32[]{:S(2)}, u32[]{:S(2)}) collective-permute-start(bf16[384,384]{1,0:T(8,128)(2,1)S(1)} %get-tuple-element.16.refs_7_), channel_id=1, source_target_pairs={{4,0},{0,4},{12,8},{8,12},{5,1},{1,5},{13,9},{9,13},{6,2},{2,6},{1... | collective-permute-start | bytes 884744 | tf_op jit(solution)/shard_map/ppermute | solution.py:342
  5.0 0.8 %shard_map.118.refs_1_ = bf16[136,256]{1,0:T(8,128)(2,1)S(1)} custom-call(bf16[8,32,256]{2,1,0:T(8,128)(2,1)} %refs_0_.3, s32[8]{0:T(128)} %lengths_ref.1), custom_call_target="tpu_custom_call" | custom-call | bytes 131104 | tf_op jit(solution)/shard_map/pallas_call | solution.py:27
  5.8 2.7 %collective-permute-start = (bf16[136,256]{1,0:T(8,128)(2,1)S(1)}, bf16[136,256]{1,0:T(8,128)(2,1)S(1)}, u32[]{:S(2)}, u32[]{:S(2)}) collective-permute-start(bf16[136,256]{1,0:T(8,128)(2,1)S(1)} %shard_map.118.refs_1_), channel_id=1, source_target_pairs={{8,0},{12,4},{0,8},{4,12},{9,1},{13,5},{1,9},{5,13},{10,2},{14,6},... | collective-permute-start | bytes 208904 | tf_op jit(solution)/shard_map/ppermute | solution.py:341
  8.5 4.3 %collective-permute-done.refs_0_ = bf16[136,256]{1,0:T(8,128)(2,1)S(1)} collective-permute-done((bf16[136,256]{1,0:T(8,128)(2,1)S(1)}, bf16[136,256]{1,0:T(8,128)(2,1)S(1)}, u32[]{:S(2)}, u32[]{:S(2)}) %collective-permute-start) | collective-permute-done | bytes 69664 | tf_op jit(solution)/shard_map/ppermute | solution.py:341
  12.8 1.5 %collective-permute-start.1 = (bf16[136,256]{1,0:T(8,128)(2,1)S(1)}, bf16[136,256]{1,0:T(8,128)(2,1)S(1)}, u32[]{:S(2)}, u32[]{:S(2)}) collective-permute-start(bf16[136,256]{1,0:T(8,128)(2,1)S(1)} %collective-permute-done.refs_0_), channel_id=1, source_target_pairs={{2,0},{0,2},{3,1},{1,3},{6,4},{4,6},{7,5},{5,7},{10,8},{8,10},{11,... | collective-permute-start | bytes 208904 | tf_op jit(solution)/shard_map/ppermute | solution.py:224
  14.3 0.5 %collective-permute-start.7 = (bf16[136,256]{1,0:T(8,128)(2,1)S(1)}, bf16[136,256]{1,0:T(8,128)(2,1)S(1)}, u32[]{:S(2)}, u32[]{:S(2)}) collective-permute-start(bf16[136,256]{1,0:T(8,128)(2,1)S(1)} %shard_map.118.refs_1_), channel_id=1, source_target_pairs={{2,0},{0,2},{3,1},{1,3},{6,4},{4,6},{7,5},{5,7},{10,8},{8,10},{11,... | collective-permute-start | bytes 208904 | tf_op jit(solution)/shard_map/ppermute | solution.py:224
  14.8 0.0 collective-permute-start.2
  14.8 2.3 %collective-permute-done.1.refs_1_ = bf16[136,256]{1,0:T(8,128)(2,1)S(1)} collective-permute-done((bf16[136,256]{1,0:T(8,128)(2,1)S(1)}, bf16[136,256]{1,0:T(8,128)(2,1)S(1)}, u32[]{:S(2)}, u32[]{:S(2)}) %collective-permute-start.1) | collective-permute-done | bytes 69664 | tf_op jit(solution)/shard_map/ppermute | solution.py:224
  17.1 0.0 collective-permute-start.3
  17.1 1.5 %collective-permute-done.7.refs_2_ = bf16[136,256]{1,0:T(8,128)(2,1)S(1)} collective-permute-done((bf16[136,256]{1,0:T(8,128)(2,1)S(1)}, bf16[136,256]{1,0:T(8,128)(2,1)S(1)}, u32[]{:S(2)}, u32[]{:S(2)}) %collective-permute-start.7) | collective-permute-done | bytes 69664 | tf_op jit(solution)/shard_map/ppermute | solution.py:224
  18.6 0.0 collective-permute-start.8
  18.6 0.0 collective-permute-done.2.refs_2_
  18.6 0.0 collective-permute-done.3.refs_3_
  18.6 0.0 copy-done.2
  18.6 0.0 copy-done.1
  18.6 0.0 copy-done.3
  18.6 1.2 %shard_map.120 = (bf16[64,384]{1,0:T(8,128)(2,1)S(1)}, bf16[512,256]{1,0:T(8,128)(2,1)S(1)}, bf16[4,256,256]{2,1,0:T(8,128)(2,1)S(1)}, f32[512,128]{1,0:T(8,128)S(1)}) custom-call(bf16[136,256]{1,0:T(8,128)(2,1)S(1)} %collective-permute-done.refs_0_, bf16[136,256]{1,0:T(8,128)(2,1)S(1)} %collective-permute-done.1.refs_1_, ...), custom_call_target="tpu_custom_call" | custom-call | flops 291504128 | bytes 917504 | tf_op jit(solution)/shard_map/pallas_call | solution.py:27
  19.8 3.4 %collective-permute-start.4 = (bf16[64,384]{1,0:T(8,128)(2,1)S(1)}, bf16[64,384]{1,0:T(8,128)(2,1)S(1)}, u32[]{:S(2)}, u32[]{:S(2)}) collective-permute-start(bf16[64,384]{1,0:T(8,128)(2,1)S(1)} %get-tuple-element.19), channel_id=1, source_target_pairs={{8,0},{12,4},{0,8},{4,12},{9,1},{13,5},{1,9},{5,13},{10,2},{14,6},... | collective-permute-start | bytes 147464 | tf_op jit(solution)/shard_map/ppermute | solution.py:346
  23.2 0.0 collective-permute-done.5.items_ref
  23.2 0.0 copy-start
  23.2 0.8 %shard_map.121 = bf16[64,384]{1,0:T(8,128)(2,1)S(1)} custom-call(bf16[384,384]{1,0:T(8,128)(2,1)S(1)} %collective-permute-done.5.items_ref, bf16[512,256]{1,0:T(8,128)(2,1)S(1)} %get-tuple-element.20.key_ref, bf16[4,256,256]{2,1,0:T(8,128)(2,1)S(1)} %get-tuple-element.21.pooled_ref, f32[512,128]{1,0:T(8,128)S(1)} %get-tuple-element.22.mask_ref, ...), custom_call_target="tpu_custom_call" | custom-call | flops 157286400 | bytes 1359872 | tf_op jit(solution)/shard_map/pallas_call | solution.py:27
  24.1 0.0 collective-permute-start.6
  24.1 0.0 collective-permute-done.8.refs_3_
  24.1 0.0 copy-done
  24.1 1.2 %shard_map.122 = (f32[8,8,384]{2,1,0:T(8,128)S(1)}, bf16[512,256]{1,0:T(8,128)(2,1)S(1)}, bf16[4,256,256]{2,1,0:T(8,128)(2,1)S(1)}, f32[512,128]{1,0:T(8,128)S(1)}) custom-call(bf16[8,32,256]{2,1,0:T(8,128)(2,1)S(1)} %copy-done, bf16[136,256]{1,0:T(8,128)(2,1)S(1)} %shard_map.118.refs_1_, bf16[136,256]{1,0:T(8,128)(2,1)S(1)} %collective-permute-done.7.refs_2_, ...), custom_call_target="tpu_custom_call" | custom-call | flops 291504128 | bytes 978944 | tf_op jit(solution)/shard_map/pallas_call | solution.py:27
  25.3 0.9 %shard_map.123.beside_ref = f32[8,8,384]{2,1,0:T(8,128)S(1)} custom-call(bf16[384,384]{1,0:T(8,128)(2,1)S(1)} %collective-permute-done.5.items_ref, bf16[512,256]{1,0:T(8,128)(2,1)S(1)} %get-tuple-element.24.key_ref, bf16[4,256,256]{2,1,0:T(8,128)(2,1)S(1)} %get-tuple-element.25.pooled_ref, f32[512,128]{1,0:T(8,128)S(1)} %get-tuple-element.26.mask_ref, ...), custom_call_target="tpu_custom_call" | custom-call | flops 157286400 | bytes 1359872 | tf_op jit(solution)/shard_map/pallas_call | solution.py:27
  26.2 0.8 %shard_map.124.refs_2_ = f32[8,9,8,384]{3,2,1,0:T(8,128)} custom-call(f32[8,8,384]{2,1,0:T(8,128)S(1)} %get-tuple-element.23.home_ref, f32[8,8,384]{2,1,0:T(8,128)S(1)} %shard_map.123.beside_ref), custom_call_target="tpu_custom_call" | custom-call | bytes 196608 | tf_op jit(solution)/shard_map/pallas_call | solution.py:27
  27.0 0.0 collective-permute-done.4.refs_0_
  27.0 2.9 %collective-permute-done.6.refs_1_ = bf16[64,384]{1,0:T(8,128)(2,1)S(1)} collective-permute-done((bf16[64,384]{1,0:T(8,128)(2,1)S(1)}, bf16[64,384]{1,0:T(8,128)(2,1)S(1)}, u32[]{:S(2)}, u32[]{:S(2)}) %collective-permute-start.6) | collective-permute-done | bytes 49184 | tf_op jit(solution)/shard_map/ppermute | solution.py:348
  29.9 0.8 %shard_map.125 = f32[8,9,8,384]{3,2,1,0:T(8,128)} custom-call(bf16[64,384]{1,0:T(8,128)(2,1)S(1)} %collective-permute-done.4.refs_0_, bf16[64,384]{1,0:T(8,128)(2,1)S(1)} %collective-permute-done.6.refs_1_, f32[8,9,8,384]{3,2,1,0:T(8,128)} %shard_map.124.refs_2_), custom_call_target="tpu_custom_call", output_to_operand_aliasing={{}: (2, {})} | custom-call | bytes 983040 | tf_op jit(solution)/shard_map/pallas_call | solution.py:27
Async XLA Ops:
  0.0 18.6 %copy-start.2 = (bf16[256,256]{1,0:T(8,128)(2,1)S(1)}, bf16[256,256]{1,0:T(8,128)(2,1)}, u32[]{:S(2)}) copy-start(bf16[256,256]{1,0:T(8,128)(2,1)} %refs_5_.3) | copy-start | bytes 393220
  1.9 16.7 %copy-start.1 = (bf16[256,256]{1,0:T(8,128)(2,1)S(1)}, bf16[256,256]{1,0:T(8,128)(2,1)}, u32[]{:S(2)}) copy-start(bf16[256,256]{1,0:T(8,128)(2,1)} %refs_4_.3) | copy-start | bytes 393220
  1.9 16.7 %copy-start.3 = (bf16[256,128]{1,0:T(8,128)(2,1)S(1)}, bf16[256,128]{1,0:T(8,128)(2,1)}, u32[]{:S(2)}) copy-start(bf16[256,128]{1,0:T(8,128)(2,1)} %refs_6_.5) | copy-start | bytes 196612
  1.9 21.3 %collective-permute-start.5 = (bf16[384,384]{1,0:T(8,128)(2,1)S(1)}, bf16[384,384]{1,0:T(8,128)(2,1)S(1)}, u32[]{:S(2)}, u32[]{:S(2)}) collective-permute-start(bf16[384,384]{1,0:T(8,128)(2,1)S(1)} %get-tuple-element.16.refs_7_), channel_id=1, source_target_pairs={{4,0},{0,4},{12,8},{8,12},{5,1},{1,5},{13,9},{9,13},{6,2},{2,6},{1... | collective-permute-start | bytes 884744 | tf_op jit(solution)/shard_map/ppermute | solution.py:342
  5.8 6.9 %collective-permute-start = (bf16[136,256]{1,0:T(8,128)(2,1)S(1)}, bf16[136,256]{1,0:T(8,128)(2,1)S(1)}, u32[]{:S(2)}, u32[]{:S(2)}) collective-permute-start(bf16[136,256]{1,0:T(8,128)(2,1)S(1)} %shard_map.118.refs_1_), channel_id=1, source_target_pairs={{8,0},{12,4},{0,8},{4,12},{9,1},{13,5},{1,9},{5,13},{10,2},{14,6},... | collective-permute-start | bytes 208904 | tf_op jit(solution)/shard_map/ppermute | solution.py:341
  12.8 4.3 %collective-permute-start.1 = (bf16[136,256]{1,0:T(8,128)(2,1)S(1)}, bf16[136,256]{1,0:T(8,128)(2,1)S(1)}, u32[]{:S(2)}, u32[]{:S(2)}) collective-permute-start(bf16[136,256]{1,0:T(8,128)(2,1)S(1)} %collective-permute-done.refs_0_), channel_id=1, source_target_pairs={{2,0},{0,2},{3,1},{1,3},{6,4},{4,6},{7,5},{5,7},{10,8},{8,10},{11,... | collective-permute-start | bytes 208904 | tf_op jit(solution)/shard_map/ppermute | solution.py:224
  14.3 4.3 %collective-permute-start.7 = (bf16[136,256]{1,0:T(8,128)(2,1)S(1)}, bf16[136,256]{1,0:T(8,128)(2,1)S(1)}, u32[]{:S(2)}, u32[]{:S(2)}) collective-permute-start(bf16[136,256]{1,0:T(8,128)(2,1)S(1)} %shard_map.118.refs_1_), channel_id=1, source_target_pairs={{2,0},{0,2},{3,1},{1,3},{6,4},{4,6},{7,5},{5,7},{10,8},{8,10},{11,... | collective-permute-start | bytes 208904 | tf_op jit(solution)/shard_map/ppermute | solution.py:224
  14.8 3.8 %collective-permute-start.2 = (bf16[136,256]{1,0:T(8,128)(2,1)S(1)}, bf16[136,256]{1,0:T(8,128)(2,1)S(1)}, u32[]{:S(2)}, u32[]{:S(2)}) collective-permute-start(bf16[136,256]{1,0:T(8,128)(2,1)S(1)} %collective-permute-done.refs_0_), channel_id=1, source_target_pairs={{1,0},{0,1},{3,2},{2,3},{5,4},{4,5},{7,6},{6,7},{9,8},{8,9},{11,10... | collective-permute-start | bytes 208904 | tf_op jit(solution)/shard_map/ppermute | solution.py:224
  17.1 1.5 %collective-permute-start.3 = (bf16[136,256]{1,0:T(8,128)(2,1)S(1)}, bf16[136,256]{1,0:T(8,128)(2,1)S(1)}, u32[]{:S(2)}, u32[]{:S(2)}) collective-permute-start(bf16[136,256]{1,0:T(8,128)(2,1)S(1)} %collective-permute-done.1.refs_1_), channel_id=1, source_target_pairs={{1,0},{0,1},{3,2},{2,3},{5,4},{4,5},{7,6},{6,7},{9,8},{8,9},{11,10... | collective-permute-start | bytes 208904 | tf_op jit(solution)/shard_map/ppermute | solution.py:224
  18.6 5.5 %collective-permute-start.8 = (bf16[136,256]{1,0:T(8,128)(2,1)S(1)}, bf16[136,256]{1,0:T(8,128)(2,1)S(1)}, u32[]{:S(2)}, u32[]{:S(2)}) collective-permute-start(bf16[136,256]{1,0:T(8,128)(2,1)S(1)} %collective-permute-done.7.refs_2_), channel_id=1, source_target_pairs={{1,0},{0,1},{3,2},{2,3},{5,4},{4,5},{7,6},{6,7},{9,8},{8,9},{11,10... | collective-permute-start | bytes 208904 | tf_op jit(solution)/shard_map/ppermute | solution.py:224
  19.8 7.2 %collective-permute-start.4 = (bf16[64,384]{1,0:T(8,128)(2,1)S(1)}, bf16[64,384]{1,0:T(8,128)(2,1)S(1)}, u32[]{:S(2)}, u32[]{:S(2)}) collective-permute-start(bf16[64,384]{1,0:T(8,128)(2,1)S(1)} %get-tuple-element.19), channel_id=1, source_target_pairs={{8,0},{12,4},{0,8},{4,12},{9,1},{13,5},{1,9},{5,13},{10,2},{14,6},... | collective-permute-start | bytes 147464 | tf_op jit(solution)/shard_map/ppermute | solution.py:346
  23.2 0.9 %copy-start = (bf16[8,32,256]{2,1,0:T(8,128)(2,1)S(1)}, bf16[8,32,256]{2,1,0:T(8,128)(2,1)}, u32[]{:S(2)}) copy-start(bf16[8,32,256]{2,1,0:T(8,128)(2,1)} %refs_0_.3) | copy-start | bytes 393220
  24.1 5.8 %collective-permute-start.6 = (bf16[64,384]{1,0:T(8,128)(2,1)S(1)}, bf16[64,384]{1,0:T(8,128)(2,1)S(1)}, u32[]{:S(2)}, u32[]{:S(2)}) collective-permute-start(bf16[64,384]{1,0:T(8,128)(2,1)S(1)} %shard_map.121), channel_id=1, source_target_pairs={{8,0},{12,4},{0,8},{4,12},{9,1},{13,5},{1,9},{5,13},{10,2},{14,6},... | collective-permute-start | bytes 147464 | tf_op jit(solution)/shard_map/ppermute | solution.py:348
where the time goes:
time: 30.9 us; the launch traced here: 30.7 us
  starting transfers between devices  11.2 us (36%)
  waiting for transfers between devices  11 us (36%)
  Pallas kernels  8.37 us (27%)
    pallas_call x8, Pallas kernels, call(): pl.pallas_call(kernel, out_shape=out_shape, in_specs=in_specs, out_specs=...  8.37 us
    ppermute x1, waiting for transfers between devices, shards(): far = lax.ppermute(piece, 'blk', across)  4.28 us
    ppermute x5, waiting for transfers between devices, shift(): lax.ppermute(block, axis, [((i + distance) % count, i) for i in range(cou...  3.78 us
    ppermute x1, starting transfers between devices, shards(): first = lax.ppermute(result, 'blk', across)  3.39 us
    ppermute x1, starting transfers between devices, shards(): other = lax.ppermute(mine, 'blk', [(i ^ 1, i) for i in range(count)])  3.12 us
    ppermute x1, waiting for transfers between devices, shards(): second = lax.ppermute(result, 'blk', across)  2.9 us
    ppermute x1, starting transfers between devices, shards(): far = lax.ppermute(piece, 'blk', across)  2.66 us
    ppermute x5, starting transfers between devices, shift(): lax.ppermute(block, axis, [((i + distance) % count, i) for i in range(cou...  2.03 us
  transfers between devices with their start and end apart: 9, of which 4 were waited for; matrix products, arithmetic and copies ran while one was open for 0% of the time, Pallas kernels for 19%

commit v1 on v0

--- a/solution.py
+++ b/solution.py
@@ -86,108 +86,201 @@
     out_ref[width:, :] = terms.T.astype(BF16)
 
 
-def keys_values(pieces, turn, w_key_ref, w_value_ref, w_pooled_ref, key_ref, pooled_ref, mask_ref, history_ref):
+def project_tokens(rows_ref, weights):
+    w_key_ref, w_value_ref, w_pooled_ref = weights
+    keys = jnp.dot(rows_ref[...], w_key_ref[...], preferred_element_type=F32).astype(BF16)
+    values = jnp.dot(rows_ref[...], w_value_ref[...], preferred_element_type=F32).astype(BF16)
+    return keys, jnp.dot(values, w_pooled_ref[...], preferred_element_type=F32)
+
+
+def arrange(pooled, firsts, lengths, state):
+    _, pooled_ref, mask_ref = state
     pairs, hid, depth = pooled_ref.shape
     hid //= 2
     both = depth - hid
     full = both // 2
-    users = 2 * pairs
-    share = users // len(pieces)
-    for s, parts in enumerate(pieces):
-        tokens = full // len(parts)
-        for r, (rows, first) in enumerate(parts):
-            at = (lax.broadcasted_iota(jnp.int32, (tokens, 128), 0) + first).astype(F32)
-            for u in range(share):
-                start = (s * share + u) * full + r * tokens
-                place = slice(start, start + tokens)
-                history_ref[place, :] = rows[u * tokens : (u + 1) * tokens]
-                mask_ref[place, :] = jnp.where(at < turn[s][u : u + 1, :128], 0.0, -jnp.inf)
-    key_ref[...] = jnp.dot(history_ref[...], w_key_ref[...], preferred_element_type=F32).astype(BF16)
-    values = jnp.dot(history_ref[...], w_value_ref[...], preferred_element_type=F32).astype(BF16)
-    pooled = jnp.dot(values, w_pooled_ref[...], preferred_element_type=F32)
+    parts = len(firsts)
+    tokens = full // parts
+    for r, first in enumerate(firsts):
+        at = (lax.broadcasted_iota(jnp.int32, (tokens, 128), 0) + first).astype(F32)
+        for user in range(2 * pairs):
+            start = user * full + r * tokens
+            valid = at < lengths[user : user + 1, :128]
+            mask_ref[start : start + tokens, :] = jnp.where(valid, 0.0, -jnp.inf)
     lane = lax.broadcasted_iota(jnp.int32, (hid, both), 1)
     one = lax.broadcasted_iota(jnp.int32, (2 * hid, hid), 0) % hid
     one = jnp.where(one == lax.broadcasted_iota(jnp.int32, (2 * hid, hid), 1), 1.0, 0.0).astype(BF16)
     for pair in range(pairs):
-        flat = pooled[pair * both : (pair + 1) * both].T
+        rows = [pooled(user, r) for user in (2 * pair, 2 * pair + 1) for r in range(parts)]
+        flat = jnp.concatenate(rows, 0).T
         pooled_ref[pair, :hid, :both] = jnp.where(lane < full, flat, 0.0).astype(BF16)
         pooled_ref[pair, hid:, :both] = jnp.where(lane < full, 0.0, flat).astype(BF16)
         pooled_ref[pair, :, both:] = one
 
 
-def score(items_ref, state, heads_ref, bias_ref, out_ref, scratch, shares):
-    key_ref, pooled_ref, mask_ref = state
+def score(items_ref, parts, states, heads_ref, bias_ref, scratch, put, late=None):
     scores_ref, weights_ref, hidden_ref = scratch
-    width = key_ref.shape[1]
-    tasks = heads_ref.shape[0] // 2
-    pairs, hid, depth = pooled_ref.shape
+    width = states[0][0].shape[1]
+    columns = items_ref.shape[1]
+    factor = math.log2(math.e) / math.sqrt(width)
+    bias = jnp.concatenate([bias_ref[...]] * (columns // 128), 1)
+    count = states[0][0].shape[0]
+    pairs, hid, depth = states[0][1].shape
     both = depth - hid // 2
     full = both // 2
-    share = pairs // shares
-    columns = items_ref.shape[1]
-    factor = math.log2(math.e) / math.sqrt(width)
-
-    scores_ref[...] = jnp.dot(key_ref[...], items_ref[:width, :], preferred_element_type=F32)
+    tokens = full // parts
+    if late:
+        early_ref, keys = late
+    else:
+        keys = jnp.concatenate([key_ref[...] for key_ref, _, _ in states], 0)
+    scores = jnp.dot(keys, items_ref[:width, :], preferred_element_type=F32)
+    scores_ref[: keys.shape[0], :] = scores
+    for at, (_, _, mask_ref) in enumerate(states):
+        for user in range(2 * pairs):
+            rows = slice(user * full, (user + 1) * full)
+            place = slice(at * count + user * full, at * count + (user + 1) * full)
+            for column in range(0, columns, 128):
+                lanes = slice(column, column + 128)
+                if late:
+                    found = [early_ref[user * tokens : (user + 1) * tokens, lanes]]
+                    for r in range(parts - 1):
+                        start = (r * 2 * pairs + user) * tokens
+                        found.append(scores_ref[start : start + tokens, lanes])
+                    scores = jnp.concatenate(found, 0)
+                else:
+                    scores = scores_ref[place, lanes]
+                scores = scores + mask_ref[rows, :]
+                maximum = jnp.max(scores, axis=0, keepdims=True)
+                expo = jnp.exp2((scores - maximum) * factor)
+                weights = expo * (1.0 / jnp.sum(expo, axis=0, keepdims=True))
+                weights_ref[place, lanes] = weights.astype(BF16)
+    turns = [(at, pair) for at in range(len(states)) for pair in range(pairs)]
+    for at, pair in turns:
+        start = at * count + pair * both
+        inputs = jnp.concatenate([weights_ref[start : start + both, :], items_ref[width:, :]], 0)
+        hidden = jnp.dot(states[at][1][pair], inputs, preferred_element_type=F32)
+        hidden_ref[at * pairs + pair] = jnp.maximum(hidden, 0.0).astype(BF16)
+    for at, pair in turns:
+        hidden = hidden_ref[at * pairs + pair]
+        put(at, pair, jnp.dot(heads_ref[...], hidden, preferred_element_type=F32) + bias)
+
+
+def keep(out_ref, shares, pairs):
+    tasks = out_ref.shape[1] if len(out_ref.shape) == 3 else None
+
+    def put(share, pair, logits):
+        user = 2 * (lax.rem(lax.axis_index("sub") + share, shares) * pairs + pair)
+        count = logits.shape[0] // 2
+        if tasks:
+            out_ref[user] = logits[:count]
+            out_ref[user + 1] = logits[count:]
+        else:
+            place = pl.multiple_of(user * count, 2 * count)
+            out_ref[pl.ds(place, 2 * count), :] = logits.astype(out_ref.dtype)
+
+    return put
+
+
+def own_kernel(shares, parts, *refs):
+    history_ref, *refs = refs
+    given = shares * parts - (shares - 1 if parts > 1 else 0)
+    pieces, refs = refs[:given], refs[given:]
+    weights, (items_ref, heads_ref, bias_ref, out_ref), refs = refs[:3], refs[3:7], refs[7:]
+    states = [tuple(refs[3 * s : 3 * s + 3]) for s in range(shares)]
+    rows_ref, *scratch = refs[3 * shares :]
+    side, me = lax.axis_index("sub"), lax.axis_index("users")
+    users, tokens, width = history_ref.shape
+    count = users // shares * tokens
+    for s in range(shares):
+        for r in range(parts):
+            if s and not r and parts > 1:
+                chosen = history_ref[pl.ds(lax.rem(side + s, shares) * (users // shares), users // shares)]
+                rows = chosen.reshape(count, width)
+            else:
+                last = pieces.pop(0)
+                rows = last[:count, :]
+            for user in range(users // shares):
+                start = (user * parts + r) * tokens
+                rows_ref[s, start : start + tokens, :] = rows[user * tokens : (user + 1) * tokens]
+        lengths = last[count:, :].astype(F32)
+        keys, values = project_tokens(rows_ref.at[s], weights)
+        states[s][0][...] = keys
+
+        def pooled(user, r):
+            start = (user * parts + r) * tokens
+            return values[start : start + tokens]
+
+        arrange(pooled, [lax.rem(me + r, parts) * tokens for r in range(parts)], lengths, states[s])
+    put = keep(out_ref, shares, states[0][1].shape[0])
+    score(items_ref, parts, states, heads_ref, bias_ref, scratch, put)
+
+
+def early_kernel(*refs):
+    *pieces, w_key_ref, w_value_ref, w_pooled_ref, items_ref = refs[:-4]
+    key_ref, values_ref, scores_ref, rows_ref = refs[-4:]
+    count = rows_ref.shape[0] // len(pieces)
+    for s, ref in enumerate(pieces):
+        rows_ref[s * count : (s + 1) * count, :] = ref[:count, :]
+    keys, values = project_tokens(rows_ref, (w_key_ref, w_value_ref, w_pooled_ref))
+    key_ref[...] = keys
+    values_ref[...] = values
+    queries = items_ref[: keys.shape[1], :]
+    scores_ref[...] = jnp.dot(keys, queries, preferred_element_type=F32)
+
+
+def share_kernel(shares, parts, share, *refs):
+    late, early, weights, refs = refs[: parts - 1], refs[parts - 1 : parts + 2], refs[parts + 2 : parts + 5], refs[parts + 5 :]
+    (items_ref, heads_ref, bias_ref), refs = refs[:3], refs[3:]
+    before = share if share == shares - 1 else 0
+    earlier, refs = refs[:before], refs[before:]
+    out_ref, state, rows_ref, scratch = refs[0], tuple(refs[1:4]), refs[4], refs[5:]
+    me, side = lax.axis_index("users"), lax.axis_index("sub")
+    count = rows_ref.shape[0] // (parts - 1)
+    pairs = state[1].shape[0]
+    tokens = count // (2 * pairs)
+    for r, ref in enumerate(late):
+        rows_ref[r * count : (r + 1) * count, :] = ref[:count, :]
+    lengths = late[-1][count:, :].astype(F32)
+    keys, values = project_tokens(rows_ref, weights)
+    held = slice(share * count, (share + 1) * count)
     for user in range(2 * pairs):
-        rows = slice(user * full, (user + 1) * full)
-        for column in range(0, columns, 128):
-            lanes = slice(column, column + 128)
-            scores = scores_ref[rows, lanes] + mask_ref[rows, :]
-            maximum = jnp.max(scores, axis=0, keepdims=True)
-            expo = jnp.exp2((scores - maximum) * factor)
-            weights = expo * (1.0 / jnp.sum(expo, axis=0, keepdims=True))
-            weights_ref[rows, lanes] = weights.astype(BF16)
-    for pair in range(pairs):
-        rows = slice(pair * both, (pair + 1) * both)
-        inputs = jnp.concatenate([weights_ref[rows, :], items_ref[width:, :]], 0)
-        hidden = jnp.dot(pooled_ref[pair], inputs, preferred_element_type=F32)
-        hidden_ref[pair] = jnp.maximum(hidden, 0.0).astype(BF16)
-    bias = jnp.concatenate([bias_ref[...]] * (columns // 128), 1)
-    for pair in range(pairs):
-        logits = jnp.dot(heads_ref[...], hidden_ref[pair], preferred_element_type=F32) + bias
-        first = lax.rem(lax.axis_index("sub") + pair // share, shares) * share + pair % share
-        if len(out_ref.shape) == 3:
-            out_ref[2 * first] = logits[:tasks]
-            out_ref[2 * first + 1] = logits[tasks:]
-        else:
-            place = pl.multiple_of(2 * first * tasks, 2 * tasks)
-            out_ref[pl.ds(place, 2 * tasks), :] = logits.astype(out_ref.dtype)
-
-
-def first_kernel(own, shares, parts, *refs):
-    if own:
-        history_ref, refs = refs[0], refs[1:]
-    given = [own and s > 0 and r == 0 and parts > 1 for s in range(shares) for r in range(parts)]
-    count = given.count(False)
-    sent, refs = list(refs[:count]), refs[count:]
-    piece_refs = [None if local else sent.pop(0) for local in given]
-    w_key_ref, w_value_ref, w_pooled_ref, items_ref, heads_ref, bias_ref = refs[:6]
-    out_ref, key_ref, pooled_ref, mask_ref, rows_ref, *scratch = refs[6:]
-    me, side = lax.axis_index("users"), lax.axis_index("sub")
-    pieces, turn = [], []
-    rows = piece_refs[0].shape[0] - LENGTH_ROWS
-    tokens = (pooled_ref.shape[2] - pooled_ref.shape[1] // 2) // 2 // parts
-    for s in range(shares):
-        entries = []
-        for r in range(parts):
-            ref = piece_refs[s * parts + r]
-            if own and s > 0 and r == 0:
-                users = history_ref.shape[0] // shares
-                chosen = history_ref[pl.ds(lax.rem(side + s, shares) * users, users)]
-                content = chosen.reshape(rows, history_ref.shape[2])
-            else:
-                content = ref[:rows, :]
-            entries.append((content, lax.rem(me + r, parts) * tokens))
-        pieces.append(entries)
-        turn.append(piece_refs[s * parts + parts - 1][rows:, :].astype(F32))
-    state = (key_ref, pooled_ref, mask_ref)
-    keys_values(pieces, turn, w_key_ref, w_value_ref, w_pooled_ref, *state, rows_ref)
-    score(items_ref, state, heads_ref, bias_ref, out_ref, scratch, shares)
-
-
-def next_kernel(shares, items_ref, key_ref, pooled_ref, mask_ref, heads_ref, bias_ref, out_ref, *scratch):
-    state = (key_ref, pooled_ref, mask_ref)
-    score(items_ref, state, heads_ref, bias_ref, out_ref, scratch, shares)
+        start = user * parts * tokens
+        first = share * count + user * tokens
+        state[0][start : start + tokens, :] = early[0][first : first + tokens, :]
+        for r in range(parts - 1):
+            start += tokens
+            first = (r * 2 * pairs + user) * tokens
+            state[0][start : start + tokens, :] = keys[first : first + tokens]
+
+    def pooled(user, r):
+        if r == 0:
+            start = share * count + user * tokens
+            return early[1][start : start + tokens, :]
+        start = ((r - 1) * 2 * pairs + user) * tokens
+        return values[start : start + tokens]
+
+    arrange(pooled, [lax.rem(me + r, parts) * tokens for r in range(parts)], lengths, state)
+    if share == shares - 1:
+        whole = keep(out_ref, shares, pairs)
+        size = out_ref.shape[0] // shares
+        for s, ref in enumerate(earlier):
+            place = pl.multiple_of(lax.rem(side + s, shares) * size, size)
+            out_ref[pl.ds(place, size), :] = ref[...]
+        put = lambda _, pair, logits: whole(share, pair, logits)
+    else:
+
+        def put(_, pair, logits):
+            size = logits.shape[0]
+            out_ref[pair * size : (pair + 1) * size, :] = logits.astype(out_ref.dtype)
+
+    score(items_ref, parts, (state,), heads_ref, bias_ref, scratch, put, (early[2].at[held, :], keys))
+
+
+def next_kernel(shares, parts, items_ref, *refs):
+    states = [tuple(refs[3 * s : 3 * s + 3]) for s in range(shares)]
+    heads_ref, bias_ref, out_ref, *scratch = refs[3 * shares :]
+    put = keep(out_ref, shares, states[0][1].shape[0])
+    score(items_ref, parts, states, heads_ref, bias_ref, scratch, put)
 
 
 def place_own_kernel(home_ref, beside_ref, out_ref, sems):
@@ -289,47 +382,49 @@
     )
     flops = 2 * users * items * (full * (width + hid) + hid * tasks)
     state = (
-        pltpu.VMEM((users * full, width), BF16),
-        pltpu.VMEM((users // 2, 2 * hid, 2 * full + hid), BF16),
-        pltpu.VMEM((users * full, 128), F32),
+        pltpu.VMEM((share * full, width), BF16),
+        pltpu.VMEM((share // 2, 2 * hid, 2 * full + hid), BF16),
+        pltpu.VMEM((share * full, 128), F32),
     )
     kept = pltpu.VMEM((users, tasks, items), F32)
     sent = pltpu.VMEM((users * tasks, items), BF16)
-    scratch = (
-        pltpu.VMEM((users * full, items), F32),
-        pltpu.VMEM((users * full, items), BF16),
-        pltpu.VMEM((users // 2, 2 * hid, items), BF16),
-    )
-
-    def start(table, block, out, own):
+    rows = pltpu.VMEM((share * full, width), BF16)
+    weights = (w_key, w_value, w_pooled)
+
+    def scratch(turns):
+        return (
+            pltpu.VMEM((turns * share * full, items), F32),
+            pltpu.VMEM((turns * share * full, items), BF16),
+            pltpu.VMEM((turns * share // 2, 2 * hid, items), BF16),
+        )
+
+    def own_start(table):
         flat = [entry for row in table for entry in row if entry is not None]
-        head = [history] if own else []
-        result = call(
-            functools.partial(first_kernel, own, shares, parts),
-            (out, *state),
-            [VMEM] * (len(head) + len(flat) + 6),
-            [VMEM] * 4,
-            (*head, *flat, w_key, w_value, w_pooled, block, heads, bias),
+        result, *states = call(
+            functools.partial(own_kernel, shares, parts),
+            (kept, *(state * shares)),
+            [VMEM] * (len(flat) + 7),
+            [VMEM] * (1 + 3 * shares),
+            (history, *flat, *weights, mine, heads, bias),
             flops + 4 * users * full * width * width,
-            (pltpu.VMEM((users * full, width), BF16), *scratch),
+            (pltpu.VMEM((shares, share * full, width), BF16), *scratch(shares)),
         )
-        return result[0], result[1:]
-
-    def go_on(held, block, out):
+        return result, states
+
+    def go_on(states, block, out):
         return call(
-            functools.partial(next_kernel, shares),
+            functools.partial(next_kernel, shares, parts),
             out,
-            [VMEM] * 6,
+            [VMEM] * (len(states) + 3),
             VMEM,
-            (block, *held, heads, bias),
+            (block, *states, heads, bias),
             flops,
-            scratch,
+            scratch(shares),
         )
 
-    if count != REACH:
+    if count != REACH or parts == 1:
         window = [None] * WIN
-        table = spread(piece, shares, parts, True)
-        window[REACH], held = start(table, mine, kept, True)
+        window[REACH], held = own_start(spread(piece, shares, parts, True))
         low = high = mine
         for offset in range(1, REACH + 1):
             low, high = shift(low, "blk", -1), shift(high, "blk", 1)
@@ -342,11 +437,38 @@
     other = lax.ppermute(mine, "blk", [(i ^ 1, i) for i in range(count)])
     table = spread(far, shares, parts)
     own = spread(piece, shares, parts, True)
-    result, guests = start(table, mine, sent, False)
+    space = share * tokens
+    early = call(
+        early_kernel,
+        (
+            pltpu.VMEM((shares * space, width), BF16),
+            pltpu.VMEM((shares * space, hid), F32),
+            pltpu.VMEM((shares * space, items), F32),
+        ),
+        [VMEM] * (shares + 4),
+        [VMEM] * 3,
+        (*(line[0] for line in table), *weights, mine),
+        flops // parts,
+        (pltpu.VMEM((shares * space, width), BF16),),
+    )
+    ready, guests = [], []
+    for s, line in enumerate(table):
+        last = s == shares - 1
+        result, *held = call(
+            functools.partial(share_kernel, shares, parts, s),
+            (sent if last else pltpu.VMEM((share * tasks, items), BF16), *state),
+            [VMEM] * (parts + 8 + (s if last else 0)),
+            [VMEM] * 4,
+            (*line[1:], *early, *weights, mine, heads, bias, *(ready if last else ())),
+            flops // shares,
+            (pltpu.VMEM(((parts - 1) * space, width), BF16), *scratch(1)),
+        )
+        ready.append(result)
+        guests += held
     first = lax.ppermute(result, "blk", across)
     result = go_on(guests, other, sent)
     second = lax.ppermute(result, "blk", across)
-    at_home, held = start(own, mine, kept, True)
+    at_home, held = own_start(own)
     beside = go_on(held, other, kept)
     whole = jax.ShapeDtypeStruct((users, WIN, tasks, items), F32)
     semaphores = pltpu.SemaphoreType.DMA((5,))

time: 30.9 us -> 31.9 us (1.032)
  Pallas kernels: 8.37 us -> 9.52 us
    pallas_call x8 -> x10, Pallas kernels: 8.37 us -> 9.52 us  [call(): pl.pallas_call(kernel, out_shape=out_shape, in_specs=in_specs, out_specs=...]
  transfers between devices with their start and end apart: 9 -> 9, of which waited for: 4 -> 4; matrix products, arithmetic and copies ran while one was open for 0% -> 0% of each run, Pallas kernels for 19% -> 22%
where the time goes in v1:
time: 31.9 us; the launch traced here: 31.7 us
  starting transfers between devices  11.2 us (35%)
  waiting for transfers between devices  10.8 us (34%)
  Pallas kernels  9.52 us (30%)
    pallas_call x10, Pallas kernels, call(): pl.pallas_call(kernel, out_shape=out_shape, in_specs=in_specs, out_specs=...  9.52 us
    ppermute x1, waiting for transfers between devices, shards(): far = lax.ppermute(piece, 'blk', across)  4.28 us
    ppermute x5, waiting for transfers between devices, shift(): lax.ppermute(block, axis, [((i + distance) % count, i) for i in range(cou...  3.78 us
    ppermute x1, starting transfers between devices, shards(): first = lax.ppermute(result, 'blk', across)  3.4 us
    ppermute x1, starting transfers between devices, shards(): other = lax.ppermute(mine, 'blk', [(i ^ 1, i) for i in range(count)])  3.12 us
    ppermute x1, waiting for transfers between devices, shards(): second = lax.ppermute(result, 'blk', across)  2.74 us
    ppermute x1, starting transfers between devices, shards(): far = lax.ppermute(piece, 'blk', across)  2.66 us
    ppermute x5, starting transfers between devices, shift(): lax.ppermute(block, axis, [((i + distance) % count, i) for i in range(cou...  2.03 us
  transfers between devices with their start and end apart: 9, of which 4 were waited for; matrix products, arithmetic and copies ran while one was open for 0% of the time, Pallas kernels for 22%

profile of v1, /device:TPU:0, one launch (start us, length us, event | category | flops | bytes accessed | tf_op | source)
XLA Modules:
  0.0 31.7 jit_solution(10972082566335478605)
XLA Ops:
  0.0 0.0 copy-start.1
  0.0 1.9 %shard_map.119 = (bf16[384,384]{1,0:T(8,128)(2,1)S(1)}, bf16[16,256]{1,0:T(8,128)(2,1)S(1)}, f32[16,128]{1,0:T(8,128)S(1)}) custom-call(bf16[384,512]{1,0:T(8,128)(2,1)} %refs_0_.2, bf16[512,256]{1,0:T(8,128)(2,1)} %refs_1_.1, bf16[512,256]{1,0:T(8,128)(2,1)} %refs_2_.2, bf16[256,128]{1,0:T(8,128)(2,1)} %refs_3_.2, f32[1,128]{1,0:T(1,128)} %bitcast.3, ...), custom_call_target="tpu_custom_call" | custom-call | flops 201326592 | bytes 985632 | tf_op jit(solution)/shard_map/pallas_call | solution.py:27
  1.9 0.0 copy-start
  1.9 0.0 copy-start.2
  1.9 3.1 %collective-permute-start.5 = (bf16[384,384]{1,0:T(8,128)(2,1)S(1)}, bf16[384,384]{1,0:T(8,128)(2,1)S(1)}, u32[]{:S(2)}, u32[]{:S(2)}) collective-permute-start(bf16[384,384]{1,0:T(8,128)(2,1)S(1)} %get-tuple-element.26.refs_5_.refs_7_), channel_id=1, source_target_pairs={{4,0},{0,4},{12,8},{8,12},{5,1},{1,5},{13,9},{9,13},{6,2},{2,6},{1... | collective-permute-start | bytes 884744 | tf_op jit(solution)/shard_map/ppermute | solution.py:437
  5.0 0.8 %shard_map.118.refs_1_ = bf16[136,256]{1,0:T(8,128)(2,1)S(1)} custom-call(bf16[8,32,256]{2,1,0:T(8,128)(2,1)} %refs_0_.3, s32[8]{0:T(128)} %lengths_ref.1), custom_call_target="tpu_custom_call" | custom-call | bytes 131104 | tf_op jit(solution)/shard_map/pallas_call | solution.py:27
  5.8 2.7 %collective-permute-start = (bf16[136,256]{1,0:T(8,128)(2,1)S(1)}, bf16[136,256]{1,0:T(8,128)(2,1)S(1)}, u32[]{:S(2)}, u32[]{:S(2)}) collective-permute-start(bf16[136,256]{1,0:T(8,128)(2,1)S(1)} %shard_map.118.refs_1_), channel_id=1, source_target_pairs={{8,0},{12,4},{0,8},{4,12},{9,1},{13,5},{1,9},{5,13},{10,2},{14,6},... | collective-permute-start | bytes 208904 | tf_op jit(solution)/shard_map/ppermute | solution.py:436
  8.5 4.3 %collective-permute-done.refs_0_ = bf16[136,256]{1,0:T(8,128)(2,1)S(1)} collective-permute-done((bf16[136,256]{1,0:T(8,128)(2,1)S(1)}, bf16[136,256]{1,0:T(8,128)(2,1)S(1)}, u32[]{:S(2)}, u32[]{:S(2)}) %collective-permute-start) | collective-permute-done | bytes 69664 | tf_op jit(solution)/shard_map/ppermute | solution.py:436
  12.8 1.5 %collective-permute-start.1 = (bf16[136,256]{1,0:T(8,128)(2,1)S(1)}, bf16[136,256]{1,0:T(8,128)(2,1)S(1)}, u32[]{:S(2)}, u32[]{:S(2)}) collective-permute-start(bf16[136,256]{1,0:T(8,128)(2,1)S(1)} %collective-permute-done.refs_0_), channel_id=1, source_target_pairs={{2,0},{0,2},{3,1},{1,3},{6,4},{4,6},{7,5},{5,7},{10,8},{8,10},{11,... | collective-permute-start | bytes 208904 | tf_op jit(solution)/shard_map/ppermute | solution.py:317
  14.3 0.5 %collective-permute-start.7 = (bf16[136,256]{1,0:T(8,128)(2,1)S(1)}, bf16[136,256]{1,0:T(8,128)(2,1)S(1)}, u32[]{:S(2)}, u32[]{:S(2)}) collective-permute-start(bf16[136,256]{1,0:T(8,128)(2,1)S(1)} %shard_map.118.refs_1_), channel_id=1, source_target_pairs={{2,0},{0,2},{3,1},{1,3},{6,4},{4,6},{7,5},{5,7},{10,8},{8,10},{11,... | collective-permute-start | bytes 208904 | tf_op jit(solution)/shard_map/ppermute | solution.py:317
  14.8 0.0 collective-permute-start.3
  14.8 2.3 %collective-permute-done.1.refs_0_ = bf16[136,256]{1,0:T(8,128)(2,1)S(1)} collective-permute-done((bf16[136,256]{1,0:T(8,128)(2,1)S(1)}, bf16[136,256]{1,0:T(8,128)(2,1)S(1)}, u32[]{:S(2)}, u32[]{:S(2)}) %collective-permute-start.1) | collective-permute-done | bytes 69664 | tf_op jit(solution)/shard_map/ppermute | solution.py:317
  17.1 0.0 collective-permute-start.2
  17.1 1.5 %collective-permute-done.7.refs_2_ = bf16[136,256]{1,0:T(8,128)(2,1)S(1)} collective-permute-done((bf16[136,256]{1,0:T(8,128)(2,1)S(1)}, bf16[136,256]{1,0:T(8,128)(2,1)S(1)}, u32[]{:S(2)}, u32[]{:S(2)}) %collective-permute-start.7) | collective-permute-done | bytes 69664 | tf_op jit(solution)/shard_map/ppermute | solution.py:317
  18.6 0.0 collective-permute-start.8
  18.6 0.0 collective-permute-done.3.refs_1_
  18.6 0.0 copy-done.1
  18.6 0.0 copy-done
  18.6 0.0 copy-done.2
  18.6 0.5 %shard_map.120 = (bf16[256,256]{1,0:T(8,128)(2,1)S(1)}, f32[256,128]{1,0:T(8,128)S(1)}, f32[256,384]{1,0:T(8,128)S(1)}) custom-call(bf16[136,256]{1,0:T(8,128)(2,1)S(1)} %collective-permute-done.refs_0_, bf16[136,256]{1,0:T(8,128)(2,1)S(1)} %collective-permute-done.3.refs_1_, bf16[256,256]{1,0:T(8,128)(2,1)S(1)} %copy-done, bf16[256,256]{1,0:T(8,128)(2,1)S(1)} %copy-done.1, ...), custom_call_target="tpu_custom_call" | custom-call | flops 78643200 | bytes 761856 | tf_op jit(solution)/shard_map/pallas_call | solution.py:27
  19.1 0.9 %shard_map.121 = (bf16[32,384]{1,0:T(8,128)(2,1)S(1)}, bf16[256,256]{1,0:T(8,128)(2,1)S(1)}, bf16[2,256,256]{2,1,0:T(8,128)(2,1)S(1)}, f32[256,128]{1,0:T(8,128)S(1)}) custom-call(bf16[136,256]{1,0:T(8,128)(2,1)S(1)} %collective-permute-done.1.refs_0_, bf16[256,256]{1,0:T(8,128)(2,1)S(1)} %get-tuple-element.27.refs_1_, ...), custom_call_target="tpu_custom_call" | custom-call | flops 78643200 | bytes 1363968 | tf_op jit(solution)/shard_map/pallas_call | solution.py:27
  19.9 0.0 collective-permute-done.2.refs_0_
  19.9 0.9 %shard_map.122 = (bf16[64,384]{1,0:T(8,128)(2,1)S(1)}, bf16[256,256]{1,0:T(8,128)(2,1)S(1)}, bf16[2,256,256]{2,1,0:T(8,128)(2,1)S(1)}, f32[256,128]{1,0:T(8,128)S(1)}) custom-call(bf16[136,256]{1,0:T(8,128)(2,1)S(1)} %collective-permute-done.2.refs_0_, bf16[256,256]{1,0:T(8,128)(2,1)S(1)} %get-tuple-element.27.refs_1_, ...), custom_call_target="tpu_custom_call" | custom-call | flops 78643200 | bytes 1388544 | tf_op jit(solution)/shard_map/pallas_call | solution.py:27
  20.8 3.4 %collective-permute-start.4 = (bf16[64,384]{1,0:T(8,128)(2,1)S(1)}, bf16[64,384]{1,0:T(8,128)(2,1)S(1)}, u32[]{:S(2)}, u32[]{:S(2)}) collective-permute-start(bf16[64,384]{1,0:T(8,128)(2,1)S(1)} %get-tuple-element.33), channel_id=1, source_target_pairs={{8,0},{12,4},{0,8},{4,12},{9,1},{13,5},{1,9},{5,13},{10,2},{14,6},... | collective-permute-start | bytes 147464 | tf_op jit(solution)/shard_map/ppermute | solution.py:468
  24.2 0.0 collective-permute-done.5.items_ref
  24.2 0.0 copy-start.3
  24.2 0.9 %shard_map.123 = bf16[64,384]{1,0:T(8,128)(2,1)S(1)} custom-call(bf16[384,384]{1,0:T(8,128)(2,1)S(1)} %collective-permute-done.5.items_ref, bf16[256,256]{1,0:T(8,128)(2,1)S(1)} %get-tuple-element.34.refs_0_, bf16[2,256,256]{2,1,0:T(8,128)(2,1)S(1)} %get-tuple-element.35.refs_1_, f32[256,128]{1,0:T(8,128)S(1)} %get-tuple-element.36.refs_2_, ...), custom_call_target="tpu_custom_call" | custom-call | flops 157286400 | bytes 1359872 | tf_op jit(solution)/shard_map/pallas_call | solution.py:27
  25.1 0.0 collective-permute-start.6
  25.1 0.0 collective-permute-done.8.refs_3_
  25.1 0.0 copy-done.3
  25.1 1.3 %shard_map.124 = (f32[8,8,384]{2,1,0:T(8,128)S(1)}, bf16[256,256]{1,0:T(8,128)(2,1)S(1)}, bf16[2,256,256]{2,1,0:T(8,128)(2,1)S(1)}, f32[256,128]{1,0:T(8,128)S(1...) custom-call(bf16[8,32,256]{2,1,0:T(8,128)(2,1)S(1)} %copy-done.3, ...), custom_call_target="tpu_custom_call" | custom-call | flops 291504128 | bytes 978944 | tf_op jit(solution)/shard_map/pallas_call | solution.py:27
  26.4 0.9 %shard_map.125.beside_ref = f32[8,8,384]{2,1,0:T(8,128)S(1)} custom-call(bf16[384,384]{1,0:T(8,128)(2,1)S(1)} %collective-permute-done.5.items_ref, bf16[256,256]{1,0:T(8,128)(2,1)S(1)} %get-tuple-element.41.refs_0_, bf16[2,256,256]{2,1,0:T(8,128)(2,1)S(1)} %get-tuple-element.42.refs_1_, f32[256,128]{1,0:T(8,128)S(1)} %get-tuple-element.43.refs_2_, ...), custom_call_target="tpu_custom_call" | custom-call | flops 157286400 | bytes 1359872 | tf_op jit(solution)/shard_map/pallas_call | solution.py:27
  27.3 0.8 %shard_map.126.refs_2_ = f32[8,9,8,384]{3,2,1,0:T(8,128)} custom-call(f32[8,8,384]{2,1,0:T(8,128)S(1)} %get-tuple-element.40.home_ref, f32[8,8,384]{2,1,0:T(8,128)S(1)} %shard_map.125.beside_ref), custom_call_target="tpu_custom_call" | custom-call | bytes 196608 | tf_op jit(solution)/shard_map/pallas_call | solution.py:27
  28.1 0.0 collective-permute-done.4.refs_0_
  28.1 2.7 %collective-permute-done.6.refs_1_ = bf16[64,384]{1,0:T(8,128)(2,1)S(1)} collective-permute-done((bf16[64,384]{1,0:T(8,128)(2,1)S(1)}, bf16[64,384]{1,0:T(8,128)(2,1)S(1)}, u32[]{:S(2)}, u32[]{:S(2)}) %collective-permute-start.6) | collective-permute-done | bytes 49184 | tf_op jit(solution)/shard_map/ppermute | solution.py:470
  30.9 0.8 %shard_map.127 = f32[8,9,8,384]{3,2,1,0:T(8,128)} custom-call(bf16[64,384]{1,0:T(8,128)(2,1)S(1)} %collective-permute-done.4.refs_0_, bf16[64,384]{1,0:T(8,128)(2,1)S(1)} %collective-permute-done.6.refs_1_, f32[8,9,8,384]{3,2,1,0:T(8,128)} %shard_map.126.refs_2_), custom_call_target="tpu_custom_call", output_to_operand_aliasing={{}: (2, {})} | custom-call | bytes 983040 | tf_op jit(solution)/shard_map/pallas_call | solution.py:27
Async XLA Ops:
  0.0 18.6 %copy-start.1 = (bf16[256,256]{1,0:T(8,128)(2,1)S(1)}, bf16[256,256]{1,0:T(8,128)(2,1)}, u32[]{:S(2)}) copy-start(bf16[256,256]{1,0:T(8,128)(2,1)} %refs_5_.5) | copy-start | bytes 393220
  1.9 16.7 %copy-start = (bf16[256,256]{1,0:T(8,128)(2,1)S(1)}, bf16[256,256]{1,0:T(8,128)(2,1)}, u32[]{:S(2)}) copy-start(bf16[256,256]{1,0:T(8,128)(2,1)} %refs_4_.7) | copy-start | bytes 393220
  1.9 16.7 %copy-start.2 = (bf16[256,128]{1,0:T(8,128)(2,1)S(1)}, bf16[256,128]{1,0:T(8,128)(2,1)}, u32[]{:S(2)}) copy-start(bf16[256,128]{1,0:T(8,128)(2,1)} %refs_6_.7) | copy-start | bytes 196612
  1.9 22.3 %collective-permute-start.5 = (bf16[384,384]{1,0:T(8,128)(2,1)S(1)}, bf16[384,384]{1,0:T(8,128)(2,1)S(1)}, u32[]{:S(2)}, u32[]{:S(2)}) collective-permute-start(bf16[384,384]{1,0:T(8,128)(2,1)S(1)} %get-tuple-element.26.refs_5_.refs_7_), channel_id=1, source_target_pairs={{4,0},{0,4},{12,8},{8,12},{5,1},{1,5},{13,9},{9,13},{6,2},{2,6},{1... | collective-permute-start | bytes 884744 | tf_op jit(solution)/shard_map/ppermute | solution.py:437
  5.8 6.9 %collective-permute-start = (bf16[136,256]{1,0:T(8,128)(2,1)S(1)}, bf16[136,256]{1,0:T(8,128)(2,1)S(1)}, u32[]{:S(2)}, u32[]{:S(2)}) collective-permute-start(bf16[136,256]{1,0:T(8,128)(2,1)S(1)} %shard_map.118.refs_1_), channel_id=1, source_target_pairs={{8,0},{12,4},{0,8},{4,12},{9,1},{13,5},{1,9},{5,13},{10,2},{14,6},... | collective-permute-start | bytes 208904 | tf_op jit(solution)/shard_map/ppermute | solution.py:436
  12.8 4.3 %collective-permute-start.1 = (bf16[136,256]{1,0:T(8,128)(2,1)S(1)}, bf16[136,256]{1,0:T(8,128)(2,1)S(1)}, u32[]{:S(2)}, u32[]{:S(2)}) collective-permute-start(bf16[136,256]{1,0:T(8,128)(2,1)S(1)} %collective-permute-done.refs_0_), channel_id=1, source_target_pairs={{2,0},{0,2},{3,1},{1,3},{6,4},{4,6},{7,5},{5,7},{10,8},{8,10},{11,... | collective-permute-start | bytes 208904 | tf_op jit(solution)/shard_map/ppermute | solution.py:317
  14.3 4.3 %collective-permute-start.7 = (bf16[136,256]{1,0:T(8,128)(2,1)S(1)}, bf16[136,256]{1,0:T(8,128)(2,1)S(1)}, u32[]{:S(2)}, u32[]{:S(2)}) collective-permute-start(bf16[136,256]{1,0:T(8,128)(2,1)S(1)} %shard_map.118.refs_1_), channel_id=1, source_target_pairs={{2,0},{0,2},{3,1},{1,3},{6,4},{4,6},{7,5},{5,7},{10,8},{8,10},{11,... | collective-permute-start | bytes 208904 | tf_op jit(solution)/shard_map/ppermute | solution.py:317
  14.8 3.8 %collective-permute-start.3 = (bf16[136,256]{1,0:T(8,128)(2,1)S(1)}, bf16[136,256]{1,0:T(8,128)(2,1)S(1)}, u32[]{:S(2)}, u32[]{:S(2)}) collective-permute-start(bf16[136,256]{1,0:T(8,128)(2,1)S(1)} %collective-permute-done.refs_0_), channel_id=1, source_target_pairs={{1,0},{0,1},{3,2},{2,3},{5,4},{4,5},{7,6},{6,7},{9,8},{8,9},{11,10... | collective-permute-start | bytes 208904 | tf_op jit(solution)/shard_map/ppermute | solution.py:317
  17.1 2.9 %collective-permute-start.2 = (bf16[136,256]{1,0:T(8,128)(2,1)S(1)}, bf16[136,256]{1,0:T(8,128)(2,1)S(1)}, u32[]{:S(2)}, u32[]{:S(2)}) collective-permute-start(bf16[136,256]{1,0:T(8,128)(2,1)S(1)} %collective-permute-done.1.refs_0_), channel_id=1, source_target_pairs={{1,0},{0,1},{3,2},{2,3},{5,4},{4,5},{7,6},{6,7},{9,8},{8,9},{11,10... | collective-permute-start | bytes 208904 | tf_op jit(solution)/shard_map/ppermute | solution.py:317
  18.6 6.5 %collective-permute-start.8 = (bf16[136,256]{1,0:T(8,128)(2,1)S(1)}, bf16[136,256]{1,0:T(8,128)(2,1)S(1)}, u32[]{:S(2)}, u32[]{:S(2)}) collective-permute-start(bf16[136,256]{1,0:T(8,128)(2,1)S(1)} %collective-permute-done.7.refs_2_), channel_id=1, source_target_pairs={{1,0},{0,1},{3,2},{2,3},{5,4},{4,5},{7,6},{6,7},{9,8},{8,9},{11,10... | collective-permute-start | bytes 208904 | tf_op jit(solution)/shard_map/ppermute | solution.py:317
  20.8 7.3 %collective-permute-start.4 = (bf16[64,384]{1,0:T(8,128)(2,1)S(1)}, bf16[64,384]{1,0:T(8,128)(2,1)S(1)}, u32[]{:S(2)}, u32[]{:S(2)}) collective-permute-start(bf16[64,384]{1,0:T(8,128)(2,1)S(1)} %get-tuple-element.33), channel_id=1, source_target_pairs={{8,0},{12,4},{0,8},{4,12},{9,1},{13,5},{1,9},{5,13},{10,2},{14,6},... | collective-permute-start | bytes 147464 | tf_op jit(solution)/shard_map/ppermute | solution.py:468
  24.2 0.9 %copy-start.3 = (bf16[8,32,256]{2,1,0:T(8,128)(2,1)S(1)}, bf16[8,32,256]{2,1,0:T(8,128)(2,1)}, u32[]{:S(2)}) copy-start(bf16[8,32,256]{2,1,0:T(8,128)(2,1)} %refs_0_.3) | copy-start | bytes 393220
  25.1 5.8 %collective-permute-start.6 = (bf16[64,384]{1,0:T(8,128)(2,1)S(1)}, bf16[64,384]{1,0:T(8,128)(2,1)S(1)}, u32[]{:S(2)}, u32[]{:S(2)}) collective-permute-start(bf16[64,384]{1,0:T(8,128)(2,1)S(1)} %shard_map.123), channel_id=1, source_target_pairs={{8,0},{12,4},{0,8},{4,12},{9,1},{13,5},{1,9},{5,13},{10,2},{14,6},... | collective-permute-start | bytes 147464 | tf_op jit(solution)/shard_map/ppermute | solution.py:470

commit v2 on v1

--- a/solution.py
+++ b/solution.py
@@ -215,26 +215,21 @@
     score(items_ref, parts, states, heads_ref, bias_ref, scratch, put)
 
 
-def early_kernel(*refs):
-    *pieces, w_key_ref, w_value_ref, w_pooled_ref, items_ref = refs[:-4]
-    key_ref, values_ref, scores_ref, rows_ref = refs[-4:]
-    count = rows_ref.shape[0] // len(pieces)
+def early_kernel(shares, *refs):
+    pieces, weights, blocks, refs = refs[:shares], refs[shares : shares + 3], refs[shares + 3 : 2 * shares + 3], refs[2 * shares + 3 :]
+    key_ref, values_ref, scores_ref, rows_ref = refs
+    count = rows_ref.shape[0] // shares
     for s, ref in enumerate(pieces):
         rows_ref[s * count : (s + 1) * count, :] = ref[:count, :]
-    keys, values = project_tokens(rows_ref, (w_key_ref, w_value_ref, w_pooled_ref))
+    keys, values = project_tokens(rows_ref, weights)
     key_ref[...] = keys
     values_ref[...] = values
-    queries = items_ref[: keys.shape[1], :]
-    scores_ref[...] = jnp.dot(keys, queries, preferred_element_type=F32)
-
-
-def share_kernel(shares, parts, share, *refs):
-    late, early, weights, refs = refs[: parts - 1], refs[parts - 1 : parts + 2], refs[parts + 2 : parts + 5], refs[parts + 5 :]
-    (items_ref, heads_ref, bias_ref), refs = refs[:3], refs[3:]
-    before = share if share == shares - 1 else 0
-    earlier, refs = refs[:before], refs[before:]
-    out_ref, state, rows_ref, scratch = refs[0], tuple(refs[1:4]), refs[4], refs[5:]
-    me, side = lax.axis_index("users"), lax.axis_index("sub")
+    queries = jnp.concatenate([ref[: keys.shape[1], :] for ref in blocks], 1)
+    scores_ref[...] = jnp.dot(keys[:count], queries, preferred_element_type=F32)
+
+
+def complete(parts, share, late, early, weights, state, rows_ref):
+    me = lax.axis_index("users")
     count = rows_ref.shape[0] // (parts - 1)
     pairs = state[1].shape[0]
     tokens = count // (2 * pairs)
@@ -242,7 +237,6 @@
         rows_ref[r * count : (r + 1) * count, :] = ref[:count, :]
     lengths = late[-1][count:, :].astype(F32)
     keys, values = project_tokens(rows_ref, weights)
-    held = slice(share * count, (share + 1) * count)
     for user in range(2 * pairs):
         start = user * parts * tokens
         first = share * count + user * tokens
@@ -260,20 +254,41 @@
         return values[start : start + tokens]
 
     arrange(pooled, [lax.rem(me + r, parts) * tokens for r in range(parts)], lengths, state)
-    if share == shares - 1:
-        whole = keep(out_ref, shares, pairs)
-        size = out_ref.shape[0] // shares
-        for s, ref in enumerate(earlier):
-            place = pl.multiple_of(lax.rem(side + s, shares) * size, size)
-            out_ref[pl.ds(place, size), :] = ref[...]
-        put = lambda _, pair, logits: whole(share, pair, logits)
-    else:
-
-        def put(_, pair, logits):
-            size = logits.shape[0]
-            out_ref[pair * size : (pair + 1) * size, :] = logits.astype(out_ref.dtype)
-
-    score(items_ref, parts, (state,), heads_ref, bias_ref, scratch, put, (early[2].at[held, :], keys))
+    return keys
+
+
+def far_kernel(shares, parts, *refs):
+    late, early, refs = refs[: parts - 1], refs[parts - 1 : parts + 2], refs[parts + 2 :]
+    weights, blocks, refs = refs[:3], refs[3 : shares + 3], refs[shares + 3 :]
+    heads_ref, bias_ref, out_ref = refs[:3]
+    state, rows_ref, scratch = tuple(refs[3:6]), refs[6], refs[7:]
+    keys = complete(parts, 0, late, early, weights, state, rows_ref)
+    items = out_ref.shape[1]
+
+    def put(_, pair, logits):
+        size = logits.shape[0]
+        for s in range(shares):
+            start = s * out_ref.shape[0] // shares + pair * size
+            part = logits[:, s * items : (s + 1) * items]
+            out_ref[start : start + size, :] = part.astype(out_ref.dtype)
+
+    queries = jnp.concatenate([ref[...] for ref in blocks], 1)
+    score(queries, parts, (state,), heads_ref, bias_ref, scratch, put, (early[2], keys))
+
+
+def far_next_kernel(shares, parts, *refs):
+    count = (shares - 1) * (parts - 1)
+    late, early, refs = refs[:count], refs[count : count + 2], refs[count + 2 :]
+    states, weights, refs = [tuple(refs[:3])], refs[3:6], refs[6:]
+    items_ref, heads_ref, bias_ref, out_ref, *refs = refs
+    scratch, refs = refs[:3], refs[3:]
+    for s in range(1, shares):
+        state, rows_ref = tuple(refs[4 * s - 4 : 4 * s - 1]), refs[4 * s - 1]
+        pieces = late[(s - 1) * (parts - 1) : s * (parts - 1)]
+        complete(parts, s, pieces, early, weights, state, rows_ref)
+        states.append(state)
+    put = keep(out_ref, shares, states[0][1].shape[0])
+    score(items_ref, parts, states, heads_ref, bias_ref, scratch, put)
 
 
 def next_kernel(shares, parts, items_ref, *refs):
@@ -294,19 +309,27 @@
         copy.wait()
 
 
-def place_away_kernel(*refs):
-    *backs, _, out_ref, held, sems = refs
+def place_away_kernel(shares, *refs):
+    firsts, (second_ref, _, out_ref, held, sems) = refs[:shares], refs[shares:]
     _, users, tasks, _ = held.shape
     odd = 3 - 2 * lax.rem(lax.axis_index("blk"), 2)
+    side = lax.axis_index("sub")
+    share = users // shares
     copies = []
-    for at, (back_ref, first) in enumerate(zip(backs, (2, odd))):
+    for at, first in enumerate((2, odd)):
         for user in range(0, users, 2):
-            both = back_ref[user * tasks : (user + 2) * tasks, :].astype(F32)
-            held[at, user] = both[:tasks]
-            held[at, user + 1] = both[tasks:]
+            if at:
+                both = second_ref[user * tasks : (user + 2) * tasks, :].astype(F32)
+                place = user
+            else:
+                s, u = user // share, user % share
+                both = firsts[s][user * tasks : (user + 2) * tasks, :].astype(F32)
+                place = lax.rem(side + shares - s, shares) * share + u
+            held[at, place] = both[:tasks]
+            held[at, place + 1] = both[tasks:]
         for k in range(2):
-            place = out_ref.at[:, first + k * REACH]
-            copies.append(pltpu.make_async_copy(held.at[at], place, sems.at[2 * at + k]))
+            target = out_ref.at[:, first + k * REACH]
+            copies.append(pltpu.make_async_copy(held.at[at], target, sems.at[2 * at + k]))
             copies[-1].start()
     for copy in copies:
         copy.wait()
@@ -435,38 +458,53 @@
     across = [(i ^ 2, i) for i in range(count)]
     far = lax.ppermute(piece, "blk", across)
     other = lax.ppermute(mine, "blk", [(i ^ 1, i) for i in range(count)])
+    blocks = [mine]
+    for turn in range(1, shares):
+        blocks.append(shift(mine, "sub", turn))
     table = spread(far, shares, parts)
     own = spread(piece, shares, parts, True)
     space = share * tokens
+    late_rows = pltpu.VMEM(((parts - 1) * space, width), BF16)
     early = call(
-        early_kernel,
+        functools.partial(early_kernel, shares),
         (
             pltpu.VMEM((shares * space, width), BF16),
             pltpu.VMEM((shares * space, hid), F32),
-            pltpu.VMEM((shares * space, items), F32),
+            pltpu.VMEM((space, shares * items), F32),
         ),
-        [VMEM] * (shares + 4),
+        [VMEM] * (2 * shares + 3),
         [VMEM] * 3,
-        (*(line[0] for line in table), *weights, mine),
+        (*(line[0] for line in table), *weights, *blocks),
         flops // parts,
         (pltpu.VMEM((shares * space, width), BF16),),
     )
-    ready, guests = [], []
-    for s, line in enumerate(table):
-        last = s == shares - 1
-        result, *held = call(
-            functools.partial(share_kernel, shares, parts, s),
-            (sent if last else pltpu.VMEM((share * tasks, items), BF16), *state),
-            [VMEM] * (parts + 8 + (s if last else 0)),
-            [VMEM] * 4,
-            (*line[1:], *early, *weights, mine, heads, bias, *(ready if last else ())),
-            flops // shares,
-            (pltpu.VMEM(((parts - 1) * space, width), BF16), *scratch(1)),
-        )
-        ready.append(result)
-        guests += held
-    first = lax.ppermute(result, "blk", across)
-    result = go_on(guests, other, sent)
+    result, *guests = call(
+        functools.partial(far_kernel, shares, parts),
+        (sent, *state),
+        [VMEM] * (parts + 7 + shares),
+        [VMEM] * 4,
+        (*table[0][1:], *early, *weights, *blocks, heads, bias),
+        flops,
+        (
+            late_rows,
+            pltpu.VMEM(((parts - 1) * space, shares * items), F32),
+            pltpu.VMEM((share * full, shares * items), BF16),
+            pltpu.VMEM((share // 2, 2 * hid, shares * items), BF16),
+        ),
+    )
+    firsts = [lax.ppermute(result, "blk", across)]
+    for turn in range(1, shares):
+        firsts.append(shift(firsts[0], "sub", -turn))
+    late = [entry for line in table[1:] for entry in line[1:]]
+    result = call(
+        functools.partial(far_next_kernel, shares, parts),
+        sent,
+        [VMEM] * (len(late) + 11),
+        VMEM,
+        (*late, *early[:2], *guests, *weights, other, heads, bias),
+        flops,
+        (*scratch(shares), *((*state, late_rows) * (shares - 1))),
+    )
     second = lax.ppermute(result, "blk", across)
     at_home, held = own_start(own)
     beside = go_on(held, other, kept)
@@ -474,8 +512,9 @@
     semaphores = pltpu.SemaphoreType.DMA((5,))
     out = call(place_own_kernel, whole, [VMEM] * 2, HBM, (at_home, beside), 0, (semaphores,))
     held = (pltpu.VMEM((2, users, tasks, items), F32), pltpu.SemaphoreType.DMA((4,)))
-    specs = [VMEM, VMEM, HBM]
-    return call(place_away_kernel, whole, specs, HBM, (first, second, out), 0, held, {2: 0})
+    specs = [VMEM] * (shares + 1) + [HBM]
+    kernel = functools.partial(place_away_kernel, shares)
+    return call(kernel, whole, specs, HBM, (*firsts, second, out), 0, held, {shares + 1: 0})
 
 
 def solution(mesh):

time: 31.9 us -> 31.9 us (level)
  Pallas kernels: 9.52 us -> 8.95 us
  waiting for transfers between devices: 10.8 us -> 11.3 us
    ppermute x1, waiting for transfers between devices: 2.74 us -> 1.28 us  [shards(): second = lax.ppermute(result, 'blk', across)]
    ppermute x1, waiting for transfers between devices: 0.01 us -> 1.31 us  [shards(): firsts = [lax.ppermute(result, 'blk', across)]]
    ppermute x1, waiting for transfers between devices: 4.28 us -> 4.88 us  [shards(): far = lax.ppermute(piece, 'blk', across)]
    pallas_call x10 -> x9, Pallas kernels: 9.52 us -> 8.95 us  [call(): pl.pallas_call(kernel, out_shape=out_shape, in_specs=in_specs, out_specs=...]
    ppermute x5 -> x7, starting transfers between devices: 2.03 us -> 2.59 us  [shift(): lax.ppermute(block, axis, [((i + distance) % count, i) for i in range(cou...]
    ppermute x1, starting transfers between devices: 3.12 us -> 2.64 us  [shards(): other = lax.ppermute(mine, 'blk', [(i ^ 1, i) for i in range(count)])]
    ppermute x5 -> x7, waiting for transfers between devices: 3.78 us -> 3.78 us  [shift(): lax.ppermute(block, axis, [((i + distance) % count, i) for i in range(cou...]
  transfers between devices with their start and end apart: 9 -> 11, of which waited for: 4 -> 5; matrix products, arithmetic and copies ran while one was open for 0% -> 0% of each run, Pallas kernels for 22% -> 20%
where the time goes in v2:
time: 31.9 us; the launch traced here: 31.7 us
  starting transfers between devices  11.3 us (35%)
  waiting for transfers between devices  11.3 us (35%)
  Pallas kernels  8.95 us (28%)
    pallas_call x9, Pallas kernels, call(): pl.pallas_call(kernel, out_shape=out_shape, in_specs=in_specs, out_specs=...  8.95 us
    ppermute x1, waiting for transfers between devices, shards(): far = lax.ppermute(piece, 'blk', across)  4.88 us
    ppermute x7, waiting for transfers between devices, shift(): lax.ppermute(block, axis, [((i + distance) % count, i) for i in range(cou...  3.78 us
    ppermute x1, starting transfers between devices, shards(): firsts = [lax.ppermute(result, 'blk', across)]  3.41 us
    ppermute x1, starting transfers between devices, shards(): far = lax.ppermute(piece, 'blk', across)  2.66 us
    ppermute x1, starting transfers between devices, shards(): other = lax.ppermute(mine, 'blk', [(i ^ 1, i) for i in range(count)])  2.64 us
    ppermute x7, starting transfers between devices, shift(): lax.ppermute(block, axis, [((i + distance) % count, i) for i in range(cou...  2.59 us
    ppermute x1, waiting for transfers between devices, shards(): firsts = [lax.ppermute(result, 'blk', across)]  1.31 us
  transfers between devices with their start and end apart: 11, of which 5 were waited for; matrix products, arithmetic and copies ran while one was open for 0% of the time, Pallas kernels for 20%

profile of v2, /device:TPU:0, one launch (start us, length us, event | category | flops | bytes accessed | tf_op | source)
XLA Modules:
  0.0 31.7 jit_solution(8859306407003644364)
XLA Ops:
  0.0 0.0 copy-start.1
  0.0 1.9 %shard_map.119 = (bf16[384,384]{1,0:T(8,128)(2,1)S(1)}, bf16[16,256]{1,0:T(8,128)(2,1)S(1)}, f32[16,128]{1,0:T(8,128)S(1)}) custom-call(bf16[384,512]{1,0:T(8,128)(2,1)} %refs_0_.2, bf16[512,256]{1,0:T(8,128)(2,1)} %refs_1_.1, bf16[512,256]{1,0:T(8,128)(2,1)} %refs_2_.2, bf16[256,128]{1,0:T(8,128)(2,1)} %refs_3_.2, f32[1,128]{1,0:T(1,128)} %bitcast.3, ...), custom_call_target="tpu_custom_call" | custom-call | flops 201326592 | bytes 985632 | tf_op jit(solution)/shard_map/pallas_call | solution.py:27
  1.9 0.0 copy-start
  1.9 0.0 copy-start.2
  1.9 0.6 %collective-permute-start.3 = (bf16[384,384]{1,0:T(8,128)(2,1)S(1)}, bf16[384,384]{1,0:T(8,128)(2,1)S(1)}, u32[]{:S(2)}, u32[]{:S(2)}) collective-permute-start(bf16[384,384]{1,0:T(8,128)(2,1)S(1)} %get-tuple-element.22.refs_5_.refs_7_), channel_id=1, source_target_pairs={{1,0},{0,1},{3,2},{2,3},{5,4},{4,5},{7,6},{6,7},{9,8},{8,9},{11,10... | collective-permute-start | bytes 884744 | tf_op jit(solution)/shard_map/ppermute | solution.py:340
  2.5 2.6 %collective-permute-start.7 = (bf16[384,384]{1,0:T(8,128)(2,1)S(1)}, bf16[384,384]{1,0:T(8,128)(2,1)S(1)}, u32[]{:S(2)}, u32[]{:S(2)}) collective-permute-start(bf16[384,384]{1,0:T(8,128)(2,1)S(1)} %get-tuple-element.22.refs_5_.refs_7_), channel_id=1, source_target_pairs={{4,0},{0,4},{12,8},{8,12},{5,1},{1,5},{13,9},{9,13},{6,2},{2,6},{1... | collective-permute-start | bytes 884744 | tf_op jit(solution)/shard_map/ppermute | solution.py:460
  5.1 0.8 %shard_map.118.refs_1_ = bf16[136,256]{1,0:T(8,128)(2,1)S(1)} custom-call(bf16[8,32,256]{2,1,0:T(8,128)(2,1)} %refs_0_.3, s32[8]{0:T(128)} %lengths_ref.1), custom_call_target="tpu_custom_call" | custom-call | bytes 131104 | tf_op jit(solution)/shard_map/pallas_call | solution.py:27
  5.9 2.7 %collective-permute-start = (bf16[136,256]{1,0:T(8,128)(2,1)S(1)}, bf16[136,256]{1,0:T(8,128)(2,1)S(1)}, u32[]{:S(2)}, u32[]{:S(2)}) collective-permute-start(bf16[136,256]{1,0:T(8,128)(2,1)S(1)} %shard_map.118.refs_1_), channel_id=1, source_target_pairs={{8,0},{12,4},{0,8},{4,12},{9,1},{13,5},{1,9},{5,13},{10,2},{14,6},... | collective-permute-start | bytes 208904 | tf_op jit(solution)/shard_map/ppermute | solution.py:459
  8.6 4.9 %collective-permute-done.refs_0_ = bf16[136,256]{1,0:T(8,128)(2,1)S(1)} collective-permute-done((bf16[136,256]{1,0:T(8,128)(2,1)S(1)}, bf16[136,256]{1,0:T(8,128)(2,1)S(1)}, u32[]{:S(2)}, u32[]{:S(2)}) %collective-permute-start) | collective-permute-done | bytes 69664 | tf_op jit(solution)/shard_map/ppermute | solution.py:459
  13.4 1.5 %collective-permute-start.1 = (bf16[136,256]{1,0:T(8,128)(2,1)S(1)}, bf16[136,256]{1,0:T(8,128)(2,1)S(1)}, u32[]{:S(2)}, u32[]{:S(2)}) collective-permute-start(bf16[136,256]{1,0:T(8,128)(2,1)S(1)} %collective-permute-done.refs_0_), channel_id=1, source_target_pairs={{2,0},{0,2},{3,1},{1,3},{6,4},{4,6},{7,5},{5,7},{10,8},{8,10},{11,... | collective-permute-start | bytes 208904 | tf_op jit(solution)/shard_map/ppermute | solution.py:340
  14.9 0.5 %collective-permute-start.9 = (bf16[136,256]{1,0:T(8,128)(2,1)S(1)}, bf16[136,256]{1,0:T(8,128)(2,1)S(1)}, u32[]{:S(2)}, u32[]{:S(2)}) collective-permute-start(bf16[136,256]{1,0:T(8,128)(2,1)S(1)} %shard_map.118.refs_1_), channel_id=1, source_target_pairs={{2,0},{0,2},{3,1},{1,3},{6,4},{4,6},{7,5},{5,7},{10,8},{8,10},{11,... | collective-permute-start | bytes 208904 | tf_op jit(solution)/shard_map/ppermute | solution.py:340
  15.5 0.0 collective-permute-start.2
  15.5 2.8 %collective-permute-done.1.refs_0_ = bf16[136,256]{1,0:T(8,128)(2,1)S(1)} collective-permute-done((bf16[136,256]{1,0:T(8,128)(2,1)S(1)}, bf16[136,256]{1,0:T(8,128)(2,1)S(1)}, u32[]{:S(2)}, u32[]{:S(2)}) %collective-permute-start.1) | collective-permute-done | bytes 69664 | tf_op jit(solution)/shard_map/ppermute | solution.py:340
  18.3 0.0 collective-permute-start.6
  18.3 0.9 %collective-permute-done.9.refs_2_ = bf16[136,256]{1,0:T(8,128)(2,1)S(1)} collective-permute-done((bf16[136,256]{1,0:T(8,128)(2,1)S(1)}, bf16[136,256]{1,0:T(8,128)(2,1)S(1)}, u32[]{:S(2)}, u32[]{:S(2)}) %collective-permute-start.9) | collective-permute-done | bytes 69664 | tf_op jit(solution)/shard_map/ppermute | solution.py:340
  19.3 0.0 collective-permute-start.10
  19.3 0.0 collective-permute-done.2.refs_1_
  19.3 0.0 collective-permute-done.3.refs_6_.refs_8_
  19.3 0.0 copy-done.1
  19.3 0.0 copy-done
  19.3 0.0 copy-done.2
  19.3 0.4 %shard_map.120 = (bf16[256,256]{1,0:T(8,128)(2,1)S(1)}, f32[256,128]{1,0:T(8,128)S(1)}, f32[128,768]{1,0:T(8,128)S(1)}) custom-call(bf16[136,256]{1,0:T(8,128)(2,1)S(1)} %collective-permute-done.refs_0_, bf16[136,256]{1,0:T(8,128)(2,1)S(1)} %collective-permute-done.2.refs_1_, bf16[256,256]{1,0:T(8,128)(2,1)S(1)} %copy-done, bf16[256,256]{1,0:T(8,128)(2,1)S(1)} %copy-done.1, ...), custom_call_target="tpu_custom_call" | custom-call | flops 78643200 | bytes 1056768 | tf_op jit(solution)/shard_map/pallas_call | solution.py:27
  19.7 1.0 %shard_map.121 = (bf16[64,384]{1,0:T(8,128)(2,1)S(1)}, bf16[256,256]{1,0:T(8,128)(2,1)S(1)}, bf16[2,256,256]{2,1,0:T(8,128)(2,1)S(1)}, f32[256,128]{1,0:T(8,128)S(1)}) custom-call(bf16[136,256]{1,0:T(8,128)(2,1)S(1)} %collective-permute-done.1.refs_0_, bf16[256,256]{1,0:T(8,128)(2,1)S(1)} %get-tuple-element.23.refs_1_, ...), custom_call_target="tpu_custom_call" | custom-call | flops 157286400 | bytes 1658880 | tf_op jit(solution)/shard_map/pallas_call | solution.py:27
  20.7 3.4 %collective-permute-start.4 = (bf16[64,384]{1,0:T(8,128)(2,1)S(1)}, bf16[64,384]{1,0:T(8,128)(2,1)S(1)}, u32[]{:S(2)}, u32[]{:S(2)}) collective-permute-start(bf16[64,384]{1,0:T(8,128)(2,1)S(1)} %get-tuple-element.28), channel_id=1, source_target_pairs={{8,0},{12,4},{0,8},{4,12},{9,1},{13,5},{1,9},{5,13},{10,2},{14,6},... | collective-permute-start | bytes 147464 | tf_op jit(solution)/shard_map/ppermute | solution.py:495
  24.1 0.0 collective-permute-done.6.refs_0_
  24.1 0.0 collective-permute-done.7.refs_9_.items_ref
  24.1 0.0 copy-start.3
  24.1 1.0 %shard_map.122 = bf16[64,384]{1,0:T(8,128)(2,1)S(1)} custom-call(bf16[136,256]{1,0:T(8,128)(2,1)S(1)} %collective-permute-done.6.refs_0_, bf16[256,256]{1,0:T(8,128)(2,1)S(1)} %get-tuple-element.23.refs_1_, f32[256,128]{1,0:T(8,128)S(1)} %get-tuple-element.24.refs_2_, bf16[256,256]{1,0:T(8,128)(2,1)S(1)} %get-tuple-element.29.refs_3_, ...), custom_call_target="tpu_custom_call" | custom-call | flops 157286400 | bytes 1495040 | tf_op jit(solution)/shard_map/pallas_call | solution.py:27
  25.2 0.0 collective-permute-start.8
  25.2 1.3 %collective-permute-done.4.refs_0_ = bf16[64,384]{1,0:T(8,128)(2,1)S(1)} collective-permute-done((bf16[64,384]{1,0:T(8,128)(2,1)S(1)}, bf16[64,384]{1,0:T(8,128)(2,1)S(1)}, u32[]{:S(2)}, u32[]{:S(2)}) %collective-permute-start.4) | collective-permute-done | bytes 49184 | tf_op jit(solution)/shard_map/ppermute | solution.py:495
  26.5 0.0 collective-permute-start.5
  26.5 0.0 collective-permute-done.10.refs_3_
  26.5 0.0 copy-done.3
  26.5 1.3 %shard_map.123 = (f32[8,8,384]{2,1,0:T(8,128)S(1)}, bf16[256,256]{1,0:T(8,128)(2,1)S(1)}, bf16[2,256,256]{2,1,0:T(8,128)(2,1)S(1)}, f32[256,128]{1,0:T(8,128)S(1...) custom-call(bf16[8,32,256]{2,1,0:T(8,128)(2,1)S(1)} %copy-done.3, ...), custom_call_target="tpu_custom_call" | custom-call | flops 291504128 | bytes 978944 | tf_op jit(solution)/shard_map/pallas_call | solution.py:27
  27.9 0.9 %shard_map.124.beside_ref = f32[8,8,384]{2,1,0:T(8,128)S(1)} custom-call(bf16[384,384]{1,0:T(8,128)(2,1)S(1)} %collective-permute-done.7.refs_9_.items_ref, bf16[256,256]{1,0:T(8,128)(2,1)S(1)} %get-tuple-element.33.refs_0_, bf16[2,256,256]{2,1,0:T(8,128)(2,1)S(1)} %get-tuple-element.34.refs_1_, f32[256,128]{1,0:T(8,128)S(1)} %get-tuple-element.35.refs_2_, ...), custom_call_target="tpu_custom_call" | custom-call | flops 157286400 | bytes 1359872 | tf_op jit(solution)/shard_map/pallas_call | solution.py:27
  28.8 0.8 %shard_map.125.refs_3_ = f32[8,9,8,384]{3,2,1,0:T(8,128)} custom-call(f32[8,8,384]{2,1,0:T(8,128)S(1)} %get-tuple-element.32.home_ref, f32[8,8,384]{2,1,0:T(8,128)S(1)} %shard_map.124.beside_ref), custom_call_target="tpu_custom_call" | custom-call | bytes 196608 | tf_op jit(solution)/shard_map/pallas_call | solution.py:27
  29.6 1.3 %collective-permute-done.8.refs_2_ = bf16[64,384]{1,0:T(8,128)(2,1)S(1)} collective-permute-done((bf16[64,384]{1,0:T(8,128)(2,1)S(1)}, bf16[64,384]{1,0:T(8,128)(2,1)S(1)}, u32[]{:S(2)}, u32[]{:S(2)}) %collective-permute-start.8) | collective-permute-done | bytes 49184 | tf_op jit(solution)/shard_map/ppermute | solution.py:508
  30.9 0.0 collective-permute-done.5.refs_1_
  30.9 0.8 %shard_map.126 = f32[8,9,8,384]{3,2,1,0:T(8,128)} custom-call(bf16[64,384]{1,0:T(8,128)(2,1)S(1)} %collective-permute-done.4.refs_0_, bf16[64,384]{1,0:T(8,128)(2,1)S(1)} %collective-permute-done.5.refs_1_, bf16[64,384]{1,0:T(8,128)(2,1)S(1)} %collective-permute-done.8.refs_2_, f32[8,9,8,384]{3,2,1,0:T(8,128)} %shard_map.125.refs_3_), custom_call_target="tpu_custom_call", output_to_operand_aliasing={{}: (3, {})} | custom-call | bytes 1032192 | tf_op jit(solution)/shard_map/pallas_call | solution.py:27
Async XLA Ops:
  0.0 19.3 %copy-start.1 = (bf16[256,256]{1,0:T(8,128)(2,1)S(1)}, bf16[256,256]{1,0:T(8,128)(2,1)}, u32[]{:S(2)}) copy-start(bf16[256,256]{1,0:T(8,128)(2,1)} %refs_5_.3) | copy-start | bytes 393220
  1.9 17.4 %copy-start = (bf16[256,256]{1,0:T(8,128)(2,1)S(1)}, bf16[256,256]{1,0:T(8,128)(2,1)}, u32[]{:S(2)}) copy-start(bf16[256,256]{1,0:T(8,128)(2,1)} %refs_4_.5) | copy-start | bytes 393220
  1.9 17.4 %copy-start.2 = (bf16[256,128]{1,0:T(8,128)(2,1)S(1)}, bf16[256,128]{1,0:T(8,128)(2,1)}, u32[]{:S(2)}) copy-start(bf16[256,128]{1,0:T(8,128)(2,1)} %refs_6_.7) | copy-start | bytes 196612
  1.9 17.4 %collective-permute-start.3 = (bf16[384,384]{1,0:T(8,128)(2,1)S(1)}, bf16[384,384]{1,0:T(8,128)(2,1)S(1)}, u32[]{:S(2)}, u32[]{:S(2)}) collective-permute-start(bf16[384,384]{1,0:T(8,128)(2,1)S(1)} %get-tuple-element.22.refs_5_.refs_7_), channel_id=1, source_target_pairs={{1,0},{0,1},{3,2},{2,3},{5,4},{4,5},{7,6},{6,7},{9,8},{8,9},{11,10... | collective-permute-start | bytes 884744 | tf_op jit(solution)/shard_map/ppermute | solution.py:340
  2.5 21.7 %collective-permute-start.7 = (bf16[384,384]{1,0:T(8,128)(2,1)S(1)}, bf16[384,384]{1,0:T(8,128)(2,1)S(1)}, u32[]{:S(2)}, u32[]{:S(2)}) collective-permute-start(bf16[384,384]{1,0:T(8,128)(2,1)S(1)} %get-tuple-element.22.refs_5_.refs_7_), channel_id=1, source_target_pairs={{4,0},{0,4},{12,8},{8,12},{5,1},{1,5},{13,9},{9,13},{6,2},{2,6},{1... | collective-permute-start | bytes 884744 | tf_op jit(solution)/shard_map/ppermute | solution.py:460
  5.9 7.5 %collective-permute-start = (bf16[136,256]{1,0:T(8,128)(2,1)S(1)}, bf16[136,256]{1,0:T(8,128)(2,1)S(1)}, u32[]{:S(2)}, u32[]{:S(2)}) collective-permute-start(bf16[136,256]{1,0:T(8,128)(2,1)S(1)} %shard_map.118.refs_1_), channel_id=1, source_target_pairs={{8,0},{12,4},{0,8},{4,12},{9,1},{13,5},{1,9},{5,13},{10,2},{14,6},... | collective-permute-start | bytes 208904 | tf_op jit(solution)/shard_map/ppermute | solution.py:459
  13.4 4.9 %collective-permute-start.1 = (bf16[136,256]{1,0:T(8,128)(2,1)S(1)}, bf16[136,256]{1,0:T(8,128)(2,1)S(1)}, u32[]{:S(2)}, u32[]{:S(2)}) collective-permute-start(bf16[136,256]{1,0:T(8,128)(2,1)S(1)} %collective-permute-done.refs_0_), channel_id=1, source_target_pairs={{2,0},{0,2},{3,1},{1,3},{6,4},{4,6},{7,5},{5,7},{10,8},{8,10},{11,... | collective-permute-start | bytes 208904 | tf_op jit(solution)/shard_map/ppermute | solution.py:340
  14.9 4.3 %collective-permute-start.9 = (bf16[136,256]{1,0:T(8,128)(2,1)S(1)}, bf16[136,256]{1,0:T(8,128)(2,1)S(1)}, u32[]{:S(2)}, u32[]{:S(2)}) collective-permute-start(bf16[136,256]{1,0:T(8,128)(2,1)S(1)} %shard_map.118.refs_1_), channel_id=1, source_target_pairs={{2,0},{0,2},{3,1},{1,3},{6,4},{4,6},{7,5},{5,7},{10,8},{8,10},{11,... | collective-permute-start | bytes 208904 | tf_op jit(solution)/shard_map/ppermute | solution.py:340
  15.5 3.8 %collective-permute-start.2 = (bf16[136,256]{1,0:T(8,128)(2,1)S(1)}, bf16[136,256]{1,0:T(8,128)(2,1)S(1)}, u32[]{:S(2)}, u32[]{:S(2)}) collective-permute-start(bf16[136,256]{1,0:T(8,128)(2,1)S(1)} %collective-permute-done.refs_0_), channel_id=1, source_target_pairs={{1,0},{0,1},{3,2},{2,3},{5,4},{4,5},{7,6},{6,7},{9,8},{8,9},{11,10... | collective-permute-start | bytes 208904 | tf_op jit(solution)/shard_map/ppermute | solution.py:340
  18.3 5.8 %collective-permute-start.6 = (bf16[136,256]{1,0:T(8,128)(2,1)S(1)}, bf16[136,256]{1,0:T(8,128)(2,1)S(1)}, u32[]{:S(2)}, u32[]{:S(2)}) collective-permute-start(bf16[136,256]{1,0:T(8,128)(2,1)S(1)} %collective-permute-done.1.refs_0_), channel_id=1, source_target_pairs={{1,0},{0,1},{3,2},{2,3},{5,4},{4,5},{7,6},{6,7},{9,8},{8,9},{11,10... | collective-permute-start | bytes 208904 | tf_op jit(solution)/shard_map/ppermute | solution.py:340
  19.3 7.3 %collective-permute-start.10 = (bf16[136,256]{1,0:T(8,128)(2,1)S(1)}, bf16[136,256]{1,0:T(8,128)(2,1)S(1)}, u32[]{:S(2)}, u32[]{:S(2)}) collective-permute-start(bf16[136,256]{1,0:T(8,128)(2,1)S(1)} %collective-permute-done.9.refs_2_), channel_id=1, source_target_pairs={{1,0},{0,1},{3,2},{2,3},{5,4},{4,5},{7,6},{6,7},{9,8},{8,9},{11,10... | collective-permute-start | bytes 208904 | tf_op jit(solution)/shard_map/ppermute | solution.py:340
  20.7 5.8 %collective-permute-start.4 = (bf16[64,384]{1,0:T(8,128)(2,1)S(1)}, bf16[64,384]{1,0:T(8,128)(2,1)S(1)}, u32[]{:S(2)}, u32[]{:S(2)}) collective-permute-start(bf16[64,384]{1,0:T(8,128)(2,1)S(1)} %get-tuple-element.28), channel_id=1, source_target_pairs={{8,0},{12,4},{0,8},{4,12},{9,1},{13,5},{1,9},{5,13},{10,2},{14,6},... | collective-permute-start | bytes 147464 | tf_op jit(solution)/shard_map/ppermute | solution.py:495
  24.1 2.4 %copy-start.3 = (bf16[8,32,256]{2,1,0:T(8,128)(2,1)S(1)}, bf16[8,32,256]{2,1,0:T(8,128)(2,1)}, u32[]{:S(2)}) copy-start(bf16[8,32,256]{2,1,0:T(8,128)(2,1)} %refs_0_.3) | copy-start | bytes 393220
  25.2 5.7 %collective-permute-start.8 = (bf16[64,384]{1,0:T(8,128)(2,1)S(1)}, bf16[64,384]{1,0:T(8,128)(2,1)S(1)}, u32[]{:S(2)}, u32[]{:S(2)}) collective-permute-start(bf16[64,384]{1,0:T(8,128)(2,1)S(1)} %shard_map.122), channel_id=1, source_target_pairs={{8,0},{12,4},{0,8},{4,12},{9,1},{13,5},{1,9},{5,13},{10,2},{14,6},... | collective-permute-start | bytes 147464 | tf_op jit(solution)/shard_map/ppermute | solution.py:508
  26.5 4.3 %collective-permute-start.5 = (bf16[64,384]{1,0:T(8,128)(2,1)S(1)}, bf16[64,384]{1,0:T(8,128)(2,1)S(1)}, u32[]{:S(2)}, u32[]{:S(2)}) collective-permute-start(bf16[64,384]{1,0:T(8,128)(2,1)S(1)} %collective-permute-done.4.refs_0_), channel_id=1, source_target_pairs={{1,0},{0,1},{3,2},{2,3},{5,4},{4,5},{7,6},{6,7},{9,8},{8,9},{11,10... | collective-permute-start | bytes 147464 | tf_op jit(solution)/shard_map/ppermute | solution.py:340
